TPU v7x, 512 devices: a whole 4x4x16 slice. The times are simulated.
512 devices in a mesh: pb: 64 (over z_lo, x, core), wa: 8 (over y, z_hi).
Axes of the slice: x: 4, y: 4, z: 16 (z_hi: 2, z_lo: 8; z = z_hi * 8 + z_lo), core: 2. Of those that a mesh axis runs over, the one named last changes fastest.
Arguments:
- psi_val: bfloat16 [16, 8, 1024], P('wa', None, 'pb'), may hold values from -0.796875 to 0.796875
- psi_cond: bfloat16 [16, 12, 1024], P('wa', None, 'pb'), may hold values from -0.796875 to 0.796875
- trials: bfloat16 [16, 1536], P('wa', 'pb'), may hold values from -6 to 6
- screened: bfloat16 [64, 1024, 1024], P('pb', 'wa'), may hold values from -0.1875 to 0.1875
- kmap: int32 [64, 16], P('pb'), may hold values from 0 to 15, each once within a row
Outputs:
- action: float32 [16, 1536], P('wa', 'pb')
Inputs may be any that keep to these rules, and one draw needn't show every extreme that they name: Every row of kmap is a permutation of the 16 k-points.
All inputs are finite; a program needn't handle non-finite values.
Results may differ from a plain program's by a relative error of at most 0.005.
Values may be sent and summed in bfloat16 or wider, within the bound.
No kernel may reach another device: no remote copies, remote signals or barrier semaphores. Data moves between devices by JAX's collectives and lax.ppermute only.
A program may use at most 64 MiB of HBM per device.

v0:
```python
import math

import jax
import jax.numpy as jnp
from jax import lax
from jax.sharding import PartitionSpec as P


def side_by_side(arrays, axis, dim, along):
    columns = [a.reshape(*a.shape[:along], -1) for a in arrays]
    both = jnp.concatenate(columns, axis=along)
    out, at, finished = (lax.all_gather(both, axis, axis=dim, tiled=True), 0, [])
    for a, column in zip(arrays, columns):
        piece = out[..., at : at + column.shape[along]]
        finished.append(piece.reshape(*piece.shape[:along], *a.shape[along:]))
        at += column.shape[along]
    return tuple(finished)


def in_order(pieces, dim):
    pieces = jnp.moveaxis(pieces, 0, dim)
    lengths = pieces.shape
    return pieces.reshape(*lengths[:dim], lengths[dim] * lengths[dim + 1], *lengths[dim + 2 :])


def one_gather(arrays, axis, dims):
    line = jnp.concatenate([a.reshape(-1) for a in arrays])
    lines, at, finished = (lax.all_gather(line, axis), 0, [])
    for a, dim in zip(arrays, dims):
        pieces = lines[:, at : at + a.size].reshape(-1, *a.shape)
        finished.append(in_order(pieces, dim))
        at += a.size
    return tuple(finished)


def split_up(x, dim, devices):
    lengths = x.shape
    pieces = x.reshape(*lengths[:dim], devices, lengths[dim] // devices, *lengths[dim + 1 :])
    return jnp.moveaxis(pieces, dim, 0)


def summed_on_arrival(x, axis, dim):
    devices = lax.axis_size(axis)
    pieces = lax.all_to_all(split_up(x, dim, devices), axis, 0, 0, tiled=True)
    return jnp.sum(pieces, axis=0)


def shards(psi_val, psi_cond, trials, screened, kmap):
    hi = lax.Precision.HIGHEST
    wa_place = lax.axis_index("wa")
    val_part, cond_part, trial_part = side_by_side((psi_val, psi_cond, trials), "wa", 0, 1)
    valence, conduct, xall = one_gather((val_part, cond_part, trial_part), "pb", (2, 2, 1))
    kcount, nval, points = valence.shape
    ncond = conduct.shape[1]
    weights = screened[0]
    pairing = kmap[0]
    nrows = weights.shape[0]
    row_start = wa_place * nrows
    ntrial = xall.shape[1] // (nval * ncond)
    xfull = xall.astype(jnp.float32).reshape(kcount, ntrial, nval, ncond)
    val_pair = valence[pairing]
    cond_pair = conduct[pairing]
    x_pair = xfull[pairing]
    block = math.gcd(kcount, 2)
    contract = (((1,), (1,)), ((), ()))

    def one_block(index):
        start = index * block
        val_here = lax.dynamic_slice_in_dim(valence, start, block, 0).astype(jnp.float32)
        val_there = lax.dynamic_slice_in_dim(val_pair, start, block, 0).astype(jnp.float32)
        cond_here = lax.dynamic_slice_in_dim(conduct, start, block, 0).astype(jnp.float32)
        cond_there = lax.dynamic_slice_in_dim(cond_pair, start, block, 0).astype(jnp.float32)
        apair = (val_here[:, :, None, :] * val_there[:, None, :, :]).astype(jnp.bfloat16)
        bpair = (cond_here[:, :, None, :] * cond_there[:, None, :, :]).astype(jnp.bfloat16)
        apair = apair.reshape(block, nval * nval, points)
        bpair = bpair.reshape(block, ncond * ncond, points)
        wa_term = lax.dot_general(
            apair.reshape(-1, points), weights, contract, preferred_element_type=jnp.float32
        )
        wb_term = lax.dot_general(
            bpair.reshape(-1, points), weights, contract, preferred_element_type=jnp.float32
        )
        wa_term = wa_term.astype(jnp.bfloat16).reshape(block, nval * nval, nrows)
        wb_term = wb_term.astype(jnp.bfloat16).reshape(block, ncond * ncond, nrows)
        a_local = lax.dynamic_slice_in_dim(apair, row_start, nrows, 2)
        b_local = lax.dynamic_slice_in_dim(bpair, row_start, nrows, 2)
        gmat = jnp.einsum("kam,kbm->kab", wa_term, b_local, preferred_element_type=jnp.float32)
        hmat = jnp.einsum("kam,kbm->kab", a_local, wb_term, preferred_element_type=jnp.float32)
        gmat = gmat.reshape(block, nval, nval, ncond, ncond)
        hmat = hmat.reshape(block, nval, nval, ncond, ncond)
        x_there = lax.dynamic_slice_in_dim(x_pair, start, block, 0)
        x_here = lax.dynamic_slice_in_dim(xfull, start, block, 0)
        forward = jnp.einsum("kvucd,ksud->ksvc", gmat, x_there, precision=hi)
        backward = jnp.einsum("kuvdc,ksud->ksvc", hmat, x_here, precision=hi)
        return (forward, backward)

    forward, backward = lax.map(one_block, jnp.arange(kcount // block, dtype=jnp.int32))
    forward = forward.reshape(kcount, ntrial, nval, ncond)
    backward = backward.reshape(kcount, ntrial, nval, ncond)
    partial_value = forward + jnp.zeros_like(forward).at[pairing].add(backward)
    flat = partial_value.reshape(kcount, ntrial * nval * ncond)
    result = summed_on_arrival(flat, "pb", 1)
    result = summed_on_arrival(result, "wa", 0)
    return result


def solution(mesh):
    in_specs = (
        P("wa", None, "pb"),
        P("wa", None, "pb"),
        P("wa", "pb"),
        P("pb", "wa", None),
        P("pb", None),
    )
    out_specs = P("wa", "pb")
    return jax.shard_map(shards, mesh=mesh, in_specs=in_specs, out_specs=out_specs, check_vma=False)
```

profile of v0, /device:TPU:1, one launch (start us, length us, event | category | flops | bytes accessed | tf_op | source)
XLA Modules:
  0.0 369.3 jit_solution(15897615974203931742)
XLA Ops:
  2.3 58.5 %all-gather.1 = bf16[8,2,344]{2,1,0:T(2,128)(2,1)S(1)} all-gather(bf16[1,2,344]{2,1,0:T(2,128)(2,1)S(1)} %maximum_bitcast_fusion), channel_id=1, replica_groups=mesh['pb'=64,'wa'=8] {'wa'}, dimensions={0}, use_global_device_ids=true | all-gather | bytes 12384 | tf_op jit(solution)/shard_map/all_gather | solution.py:12
  61.1 131.9 %all-gather.2 = bf16[64,1,5504]{2,1,0:T(2,128)(2,1)S(1)} all-gather(bf16[1,1,5504]{2,1,0:T(2,128)(2,1)S(1)} %reshape.175), channel_id=2, replica_groups=mesh['pb'=64,'wa'=8] {'pb'}, dimensions={0}, use_global_device_ids=true | all-gather | bytes 715520 | tf_op jit(solution)/shard_map/all_gather | solution.py:28
  195.7 1.9 copy.86
  197.6 3.6 reshape.132
  205.3 2.8 copy.102
  208.1 5.9 %reshape.182 = bf16[16,12,1024]{2,1,0:T(8,128)(2,1)} reshape(bf16[16,12,64,16]{3,2,1,0:T(8,128)(2,1)S(1)} %copy.102) | data formatting | bytes 786432 | tf_op jit(solution)/shard_map/while | solution.py:97
  215.6 107.0 %while.14 = (s32[]{:T(128)}, f32[8,2,16,8,12]{2,3,4,1,0:T(8,128)}, f32[8,2,16,8,12]{4,2,3,1,0:T(8,128)}, s32[8]{0:T(128)S(1)}, f32[16,16,8,12]{3,2,1,0:T(8,128)}...) while((s32[]{:T(128)}, f32[8,2,16,8,12]{2,3,4,1,0:T(8,128)}, ...), condition=%wide.region_1.2_spmd, body=%wide.region_0.1_spmd.sunk | while | flops 126554112 | bytes 7078131 | solution.py:97
  221.5 3.7 %convolution_bitcast_fusion.3 = f32[1,2,16,8,12]{4,2,3,1,0:T(8,128)S(1)} fusion(f32[2,8,8,12,12]{4,3,2,1,0:T(8,128)S(1)} %reshape.187, f32[2,16,8,12]{3,2,1,0:T(8,128)S(1)} %get-tuple-element.326), kind=kOutput, calls=%fused_computation.7.clone.1 | convolution fusion | flops 3538944 | bytes 98304 | tf_op jit(solution)/shard_map/while/body/eval_jaxpr/kvucd,ksud->ksvc/dot_general | solution.py:93
  227.2 1.9 fusion.47
  234.8 3.7 %convolution_bitcast_fusion.3 = f32[1,2,16,8,12]{4,2,3,1,0:T(8,128)S(1)} fusion(f32[2,8,8,12,12]{4,3,2,1,0:T(8,128)S(1)} %reshape.187, f32[2,16,8,12]{3,2,1,0:T(8,128)S(1)} %get-tuple-element.326), kind=kOutput, calls=%fused_computation.7.clone.1 | convolution fusion | flops 3538944 | bytes 98304 | tf_op jit(solution)/shard_map/while/body/eval_jaxpr/kvucd,ksud->ksvc/dot_general | solution.py:93
  240.5 1.9 fusion.47
  248.2 3.7 %convolution_bitcast_fusion.3 = f32[1,2,16,8,12]{4,2,3,1,0:T(8,128)S(1)} fusion(f32[2,8,8,12,12]{4,3,2,1,0:T(8,128)S(1)} %reshape.187, f32[2,16,8,12]{3,2,1,0:T(8,128)S(1)} %get-tuple-element.326), kind=kOutput, calls=%fused_computation.7.clone.1 | convolution fusion | flops 3538944 | bytes 98304 | tf_op jit(solution)/shard_map/while/body/eval_jaxpr/kvucd,ksud->ksvc/dot_general | solution.py:93
  261.6 3.7 %convolution_bitcast_fusion.3 = f32[1,2,16,8,12]{4,2,3,1,0:T(8,128)S(1)} fusion(f32[2,8,8,12,12]{4,3,2,1,0:T(8,128)S(1)} %reshape.187, f32[2,16,8,12]{3,2,1,0:T(8,128)S(1)} %get-tuple-element.326), kind=kOutput, calls=%fused_computation.7.clone.1 | convolution fusion | flops 3538944 | bytes 98304 | tf_op jit(solution)/shard_map/while/body/eval_jaxpr/kvucd,ksud->ksvc/dot_general | solution.py:93
  267.3 1.9 fusion.47
  275.0 3.7 %convolution_bitcast_fusion.3 = f32[1,2,16,8,12]{4,2,3,1,0:T(8,128)S(1)} fusion(f32[2,8,8,12,12]{4,3,2,1,0:T(8,128)S(1)} %reshape.187, f32[2,16,8,12]{3,2,1,0:T(8,128)S(1)} %get-tuple-element.326), kind=kOutput, calls=%fused_computation.7.clone.1 | convolution fusion | flops 3538944 | bytes 98304 | tf_op jit(solution)/shard_map/while/body/eval_jaxpr/kvucd,ksud->ksvc/dot_general | solution.py:93
  288.3 3.7 %convolution_bitcast_fusion.3 = f32[1,2,16,8,12]{4,2,3,1,0:T(8,128)S(1)} fusion(f32[2,8,8,12,12]{4,3,2,1,0:T(8,128)S(1)} %reshape.187, f32[2,16,8,12]{3,2,1,0:T(8,128)S(1)} %get-tuple-element.326), kind=kOutput, calls=%fused_computation.7.clone.1 | convolution fusion | flops 3538944 | bytes 98304 | tf_op jit(solution)/shard_map/while/body/eval_jaxpr/kvucd,ksud->ksvc/dot_general | solution.py:93
  294.0 1.9 fusion.47
  301.7 3.7 %convolution_bitcast_fusion.3 = f32[1,2,16,8,12]{4,2,3,1,0:T(8,128)S(1)} fusion(f32[2,8,8,12,12]{4,3,2,1,0:T(8,128)S(1)} %reshape.187, f32[2,16,8,12]{3,2,1,0:T(8,128)S(1)} %get-tuple-element.326), kind=kOutput, calls=%fused_computation.7.clone.1 | convolution fusion | flops 3538944 | bytes 98304 | tf_op jit(solution)/shard_map/while/body/eval_jaxpr/kvucd,ksud->ksvc/dot_general | solution.py:93
  307.4 1.9 fusion.47
  315.1 3.7 %convolution_bitcast_fusion.3 = f32[1,2,16,8,12]{4,2,3,1,0:T(8,128)S(1)} fusion(f32[2,8,8,12,12]{4,3,2,1,0:T(8,128)S(1)} %reshape.187, f32[2,16,8,12]{3,2,1,0:T(8,128)S(1)} %get-tuple-element.326), kind=kOutput, calls=%fused_computation.7.clone.1 | convolution fusion | flops 3538944 | bytes 98304 | tf_op jit(solution)/shard_map/while/body/eval_jaxpr/kvucd,ksud->ksvc/dot_general | solution.py:93
  320.8 1.9 fusion.47
  322.7 2.1 copy.94
  328.2 16.9 %all_to_all.10 = f32[64,1,384]{2,1,0:T(1,128)S(1)} all-to-all(f32[64,1,384]{2,1,0:T(1,128)S(1)} %reshape.183), channel_id=1, replica_groups=mesh['pb'=64,'wa'=8] {'pb'}, dimensions={0} | all-to-all | bytes 196608 | tf_op jit(solution)/shard_map/all_to_all | solution.py:44
  346.9 21.8 %all_to_all.11 = f32[8,2,24]{2,1,0:T(2,128)S(1)} all-to-all(f32[8,2,24]{2,1,0:T(2,128)S(1)} %bitcast.120), channel_id=1, replica_groups=mesh['pb'=64,'wa'=8] {'wa'}, dimensions={0} | all-to-all | bytes 3072 | tf_op jit(solution)/shard_map/all_to_all | solution.py:44
  (189 shorter events, 76.2 us)
Async XLA Ops:
  193.2 1.3 copy-start.5
  194.5 6.6 %copy-start.1 = (f32[16,16,8,12]{3,2,1,0:T(8,128)}, f32[16,16,8,12]{3,2,1,0:T(8,128)S(1)}, u32[]{:S(2)}) copy-start(f32[16,16,8,12]{3,2,1,0:T(8,128)S(1)} %reshape.138) | copy-start | bytes 294916
  201.2 4.1 %copy-start.3 = (bf16[16,8,1024]{2,1,0:T(8,128)(2,1)}, bf16[16,8,1024]{2,1,0:T(8,128)(2,1)S(1)}, u32[]{:S(2)}) copy-start(bf16[16,8,1024]{2,1,0:T(8,128)(2,1)S(1)} %reshape.132) | copy-start | bytes 786436
  201.2 2.9 copy-start.4
  208.1 7.5 %copy-start = (bf16[1,128,1024]{2,1,0:T(8,128)(2,1)S(1)}, bf16[1,128,1024]{2,1,0:T(8,128)(2,1)}, u32[]{:S(2)}) copy-start(bf16[1,128,1024]{2,1,0:T(8,128)(2,1)} %param.10) | copy-start | bytes 786436
  322.6 2.1 copy-start.2
where the time goes:
time: 371 us; the launch traced here: 369 us
  blocking collectives  229 us (62%)
  local copies, waits for them, and re-layouts  63.1 us (17%)
  matrix products  52 us (14%)
  other arithmetic  18.6 us (5%)
  loops' own time  6.3 us (2%)
    all_gather x1, blocking collectives, one_gather(): lines, at, finished = (lax.all_gather(line, axis), 0, [])  132 us
    all_gather x1, blocking collectives, side_by_side(): lax.all_gather(both, axis, axis=dim, tiled=True)  58.5 us
    all_to_all x2, blocking collectives, summed_on_arrival(): pieces = lax.all_to_all(split_up(x, dim, devices), axis, 0, 0, tiled=True)  38.7 us
    dot_general x8, matrix products, one_block(): forward = jnp.einsum('kvucd,ksud->ksvc', gmat, x_there, precision=hi)  30 us
    dot_general x8, matrix products, one_block(): backward = jnp.einsum('kuvdc,ksud->ksvc', hmat, x_here, precision=hi)  15 us
    while x2, local copies, waits for them, and re-layouts, shards(): lax.map(one_block, jnp.arange(kcount // block, dtype=jnp.int32))  8.71 us
    dynamic_slice x8, local copies, waits for them, and re-layouts, one_block(): x_here = lax.dynamic_slice_in_dim(xfull, start, block, 0)  7.95 us

commit v1 on v0

v1 whole, which is shorter than its diff:
```python
import itertools

import jax
import jax.numpy as jnp
from jax import lax
from jax.experimental import pallas as pl
from jax.experimental.pallas import tpu as pltpu
from jax.sharding import PartitionSpec as P

AXES = ("pb", "wa")
NX, NY, NZ, NC = 4, 4, 16, 2
F32 = jnp.float32
BF16 = jnp.bfloat16


def place(x, y, z, c):
    return (((z % 8) * NX + x) * NC + c) * 8 + y * 2 + z // 8


def lines():
    spans = itertools.product(range(NX), range(NY), range(NC))
    return [[place(x, y, z, c) for z in range(NZ)] for x, y, c in spans]


def planes():
    spots = list(itertools.product(range(NY), range(NX), range(NC)))
    return [[place(x, y, z, c) for y, x, c in spots] for z in range(NZ)]


def swap_kernel(in_ref, out_ref, wide):
    wide[...] = in_ref[...].astype(F32).reshape(128, 128)
    row = lax.broadcasted_iota(jnp.int32, (8, 128), 0)
    lane = lax.broadcasted_iota(jnp.int32, (8, 128), 1) // 16
    turn = lax.rem(row - lane + 8, 8)
    tiles = []
    for zh in range(2):
        for a in range(6):
            tile = wide[pl.ds(zh * 64 + a, 8, stride=8), :]
            done = jnp.where(turn == 0, tile, 0.0)
            for step in range(1, 8):
                moved = pltpu.roll(pltpu.roll(tile, step, 0), 128 - 16 * step, 1)
                done = jnp.where(turn == step, moved, done)
            tiles.append(done)
    block = jnp.concatenate(tiles, axis=0).astype(BF16)
    for dest in range(out_ref.shape[0]):
        out_ref[dest] = block


def swap(x):
    return pl.pallas_call(
        swap_kernel,
        out_shape=jax.ShapeDtypeStruct((32, 96, 128), BF16),
        in_specs=[pl.BlockSpec(memory_space=pltpu.VMEM)],
        out_specs=pl.BlockSpec(memory_space=pltpu.VMEM),
        scratch_shapes=[pltpu.VMEM((128, 128), F32)],
        name="swap",
    )(x)


NT = (((1,), (1,)), ((), ()))


def main_kernel(
    kmap_ref, spot_ref, r_ref, w_ref, o_ref, wt, psi, loc, t1, t2, ww, lf, acc, back
):
    spot = spot_ref[0]
    lane16 = lax.broadcasted_iota(jnp.int32, (8, 128), 1) // 16
    sub8 = lax.broadcasted_iota(jnp.int32, (8, 128), 0)
    own = lane16 == sub8

    for z in range(8):
        turned = w_ref[:, z * 128 : (z + 1) * 128].astype(F32).T.astype(BF16)
        for xc in range(8):
            wt[xc * 128 + z * 16 : xc * 128 + (z + 1) * 16, :] = turned[
                xc * 16 : (xc + 1) * 16
            ]
    acc[...] = jnp.zeros_like(acc)
    back[...] = jnp.zeros_like(back)

    lane24 = lax.broadcasted_iota(jnp.int32, (24, 128), 1) // 16

    def spread(k, carry):
        y, k4 = k // 4, lax.rem(k, 4)
        local = jnp.zeros((24, 128), F32)
        for xc in range(8):
            tile = r_ref[y, xc, k4].astype(F32)
            psi[k, :, xc * 128 : (xc + 1) * 128] = tile
            shift = lax.rem((xc - spot + 8) * 16, 128)
            local = jnp.where(lane24 == xc, pltpu.roll(tile, shift, 1), local)
        loc[k] = local
        rows, cols = [], []
        for u in range(8):
            for xh in range(2):
                xc = xh * 4 + u // 2
                at = psi[k, 20 + u % 2 : 21 + u % 2, xc * 128 : (xc + 1) * 128]
                rows.append(jnp.where(own, jnp.broadcast_to(at, (8, 128)), 0.0))
        left = jnp.concatenate(rows, axis=0).astype(BF16)
        right = jnp.concatenate([local[8:24]] * 8, axis=0).astype(BF16)
        t1[k] = jnp.dot(left, right, preferred_element_type=F32)
        for xh in range(2):
            x8 = jnp.concatenate(
                [
                    psi[k, 20:22, (xh * 4 + i) * 128 : (xh * 4 + i + 1) * 128]
                    for i in range(4)
                ],
                axis=0,
            )
            t2[k, xh] = jnp.dot(
                x8.T.astype(BF16), local[0:8].astype(BF16), preferred_element_type=F32
            )
        return carry

    lax.fori_loop(0, 16, spread, 0)

    def pair(k, carry):
        p = kmap_ref[k]
        val_here = psi[k, 0:8, :]
        cond_there = psi[p, 8:24, :]
        parts = [psi[p, u : u + 1, :] * val_here for u in range(8)]
        parts += [psi[k, 8 + d : 9 + d, :] * cond_there for d in range(12)]
        pairs = jnp.concatenate([part.astype(BF16) for part in parts], axis=0)
        ww[...] = jnp.dot(pairs, wt[...], preferred_element_type=F32)

        left = jnp.concatenate(
            [ww[u * 8 : (u + 1) * 8, :].astype(BF16) for u in range(8)], axis=1
        )
        for xh in range(2):
            for u in range(8):
                tile = t1[p, (u * 2 + xh) * 8 : (u * 2 + xh + 1) * 8, :]
                grown = [
                    tile * jnp.broadcast_to(loc[k, 8 + c : 9 + c, :], (8, 128))
                    for c in range(12)
                ]
                lf[:, u * 128 : (u + 1) * 128] = jnp.concatenate(grown, axis=0).astype(
                    BF16
                )
            base = (k * 2 + xh) * 8
            acc[pl.ds(pl.multiple_of(base, 8), 8), 0:96] = lax.dot_general(
                left, lf[...], NT, preferred_element_type=F32
            )
        val_there = loc[p, 0:8, :].astype(BF16)
        for xh in range(2):
            cols = [t2[k, xh, pl.ds(d, 8, stride=16), :] for d in range(12)]
            sums = []
            for c in range(12):
                total = cols[0] * jnp.broadcast_to(ww[64 + c : 65 + c, :], (8, 128))
                for d in range(1, 12):
                    at = 64 + d * 16 + c
                    total += cols[d] * jnp.broadcast_to(ww[at : at + 1, :], (8, 128))
                sums.append(total)
            right = jnp.concatenate(sums, axis=0).astype(BF16)
            base = (p * 2 + xh) * 8
            back[pl.ds(pl.multiple_of(base, 8), 8), 0:96] = lax.dot_general(
                val_there, right, NT, preferred_element_type=F32
            )
        return carry

    lax.fori_loop(0, 16, pair, 0)

    acc[...] += back[...]
    for y in range(4):
        for xc in range(8):
            for ih in range(2):
                at = (y * 8 + xc // 4) * 8 + (xc % 4) * 2 + ih
                o_ref[y * 8 + xc, ih * 4 : (ih + 1) * 4, :] = acc[
                    pl.ds(at, 4, stride=16), :
                ]


def main(pairing, spot, gathered, weights):
    vmem = pl.BlockSpec(memory_space=pltpu.VMEM)
    smem = pl.BlockSpec(memory_space=pltpu.SMEM)
    return pl.pallas_call(
        main_kernel,
        out_shape=jax.ShapeDtypeStruct((32, 8, 128), F32),
        in_specs=[smem, smem, vmem, vmem],
        out_specs=vmem,
        scratch_shapes=[
            pltpu.VMEM((1024, 128), BF16),
            pltpu.VMEM((16, 24, 1024), F32),
            pltpu.VMEM((16, 24, 128), F32),
            pltpu.VMEM((16, 128, 128), F32),
            pltpu.VMEM((16, 2, 128, 128), F32),
            pltpu.VMEM((256, 128), F32),
            pltpu.VMEM((96, 1024), BF16),
            pltpu.VMEM((256, 128), F32),
            pltpu.VMEM((256, 128), F32),
        ],
        name="act",
    )(pairing, spot, gathered, weights)


def shards(psi_val, psi_cond, trials, screened, kmap):
    extra = jnp.pad(trials.reshape(2, 2, 12), ((0, 0), (0, 2), (0, 4)))
    line = jnp.concatenate([psi_val, psi_cond, extra], axis=1).reshape(6, 128)
    line = jnp.pad(line, ((0, 2), (0, 0)))
    along = lax.all_to_all(
        jnp.broadcast_to(line, (16, 8, 128)),
        AXES,
        0,
        0,
        tiled=True,
        axis_index_groups=lines(),
    )
    across = lax.all_to_all(
        swap(along), AXES, 0, 0, tiled=True, axis_index_groups=planes()
    )
    spot = lax.axis_index("wa").reshape(1)
    sums = main(
        kmap.reshape(16), spot, across.reshape(4, 8, 4, 24, 128), screened[0]
    )
    sums = lax.all_to_all(sums, AXES, 0, 0, tiled=True, axis_index_groups=planes())
    sums = jnp.sum(sums, axis=0)[:, :96].reshape(2, 2, 2, 12, 8)
    sums = sums.transpose(1, 4, 2, 0, 3).reshape(16, 48)
    sums = lax.all_to_all(sums, AXES, 0, 0, tiled=True, axis_index_groups=lines())
    return jnp.sum(sums, axis=0).reshape(2, 24)


def solution(mesh):
    in_specs = (
        P("wa", None, "pb"),
        P("wa", None, "pb"),
        P("wa", "pb"),
        P("pb", "wa", None),
        P("pb", None),
    )
    return jax.shard_map(
        shards, mesh=mesh, in_specs=in_specs, out_specs=P("wa", "pb"), check_vma=False
    )
```

time: 371 us -> 96.3 us (0.26)
  blocking collectives: 229 us -> 52.7 us
  local copies, waits for them, and re-layouts: 63.1 us -> 2.75 us
  matrix products: 52 us -> 0 us
  other arithmetic: 18.6 us -> 0.09 us
  Pallas kernels: 0 us -> 16.9 us
  waiting for transfers between devices: 0 us -> 14.2 us
  starting transfers between devices: 0 us -> 9.13 us
  loops' own time: 6.3 us -> 0 us
    all_gather x2 -> x0, blocking collectives: 190 us -> none  [the longest x1 132 us: one_gather(): lines, at, finished = (lax.all_gather(line, axis), 0, [])]
    dot_general x48 -> x0, matrix products: 52 us -> none  [the longest x8 30 us: one_block(): forward = jnp.einsum('kvucd,ksud->ksvc', gmat, x_there, precision=hi)]
    pallas_call x0 -> x2, Pallas kernels: none -> 16.9 us  [the longest x1 15.1 us: main(): pl.pallas_call(main_kernel, out_shape=jax.ShapeDtypeStruct((32, 8, 128),...]
    convert_element_type x33 -> x0, other arithmetic: 14.6 us -> none  [the longest x8 6.93 us: one_block(): lax.dynamic_slice_in_dim(cond_pair, start, block, 0).astype(jnp.float32)]
    all_to_all x0 -> x1, waiting for transfers between devices: none -> 14.2 us  [shards(): lax.all_to_all(swap(along), AXES, 0, 0, tiled=True, axis_index_groups=pla...]
    all_to_all x2 -> x3, blocking collectives: 38.7 us -> 52.7 us  [the longest x1 27.1 us: shards(): lax.all_to_all(jnp.broadcast_to(line, (16, 8, 128)), AXES, 0, 0, tiled=Tr...]
    dynamic_slice x24 -> x0, local copies, waits for them, and re-layouts: 13.7 us -> none  [the longest x8 7.95 us: one_block(): x_here = lax.dynamic_slice_in_dim(xfull, start, block, 0)]
    reshape x21 -> x4, local copies, waits for them, and re-layouts: 14.4 us -> 0.9 us  [the longest x1 0.65 us: shards(): return jnp.sum(sums, axis=0).reshape(2, 24)]
  transfers between devices with their start and end apart: 0 -> 1, of which waited for: 0 -> 1; matrix products, arithmetic and copies ran while one was open for 0% -> 0% of each run, Pallas kernels for 0% -> 0%
where the time goes in v1:
time: 96.3 us; the launch traced here: 95.8 us
  blocking collectives  52.7 us (55%)
  Pallas kernels  16.9 us (18%)
  waiting for transfers between devices  14.2 us (15%)
  starting transfers between devices  9.13 us (9%)
  local copies, waits for them, and re-layouts  2.75 us (3%)
    all_to_all x1, blocking collectives, shards(): lax.all_to_all(jnp.broadcast_to(line, (16, 8, 128)), AXES, 0, 0, tiled=Tr...  27.1 us
    pallas_call x1, Pallas kernels, main(): pl.pallas_call(main_kernel, out_shape=jax.ShapeDtypeStruct((32, 8, 128),...  15.1 us
    all_to_all x1, waiting for transfers between devices, shards(): lax.all_to_all(swap(along), AXES, 0, 0, tiled=True, axis_index_groups=pla...  14.2 us
    all_to_all x1, blocking collectives, shards(): lax.all_to_all(sums, AXES, 0, 0, tiled=True, axis_index_groups=lines())  13.8 us
    all_to_all x1, blocking collectives, shards(): lax.all_to_all(sums, AXES, 0, 0, tiled=True, axis_index_groups=planes())  11.7 us
    all_to_all x1, starting transfers between devices, shards(): lax.all_to_all(swap(along), AXES, 0, 0, tiled=True, axis_index_groups=pla...  9.13 us
  transfers between devices with their start and end apart: 1, of which 1 were waited for; matrix products, arithmetic and copies ran while one was open for 0% of the time, Pallas kernels for 0%

profile of v1, /device:TPU:1, one launch (start us, length us, event | category | flops | bytes accessed | tf_op | source)
XLA Modules:
  0.0 95.8 jit_solution(4051028172451647553)
XLA Ops:
  0.0 0.0 copy-start.2
  0.0 0.0 copy-start.1
  0.0 0.7 copy.12
  0.7 0.0 copy-done.2
  0.7 0.1 reshape.27
  0.8 0.0 copy-done.1
  0.9 0.1 reshape.28
  1.0 27.1 %all_to_all.24.in_ref = bf16[16,8,128]{2,1,0:T(8,128)(2,1)} all-to-all(bf16[16,8,128]{2,1,0:T(8,128)(2,1)S(1)} %broadcast_in_dim.3), channel_id=1, replica_groups={{0,64,128,192,256,320,384,448,1,65,129,193,257,321,385,449},{8,72,136,2..., dimensions={0} | all-to-all | bytes 65536 | tf_op jit(solution)/shard_map/all_to_all | solution.py:197
  28.1 1.8 %swap.1 = bf16[32,96,128]{2,1,0:T(8,128)(2,1)} custom-call(bf16[16,8,128]{2,1,0:T(8,128)(2,1)} %all_to_all.24.in_ref), custom_call_target="tpu_custom_call" | custom-call | tf_op jit(solution)/shard_map/swap/pallas_call | solution.py:50
  29.9 9.1 %all-to-all-start.1 = ((bf16[32,96,128]{2,1,0:T(8,128)(2,1)}), bf16[32,96,128]{2,1,0:T(8,128)(2,1)S(1)}, u32[]{:S(2)}, u32[]{:S(2)}) async-start(bf16[32,96,128]{2,1,0:T(8,128)(2,1)} %swap.1), calls=%async_computation.1 | async-start | bytes 1572864 | tf_op jit(solution)/shard_map/all_to_all | solution.py:205
  39.0 14.2 %all-to-all-done.1 = bf16[32,96,128]{2,1,0:T(8,128)(2,1)S(1)} async-done(((bf16[32,96,128]{2,1,0:T(8,128)(2,1)}), bf16[32,96,128]{2,1,0:T(8,128)(2,1)S(1)}, u32[]{:S(2)}, u32[]{:S(2)}) %all-to-all-start.1) | async-done | bytes 786464 | tf_op jit(solution)/shard_map/all_to_all | solution.py:205
  53.2 0.0 copy-start
  53.2 0.9 copy-done
  54.1 15.1 %act.1 = f32[32,8,128]{2,1,0:T(8,128)} custom-call(s32[16]{0:T(128)} %bitcast.12, s32[1]{0:T(128)} %bitcast.1.spot_ref, bf16[4,8,4,24,128]{4,3,2,1,0:T(8,128)(2,1)} %bitcast.7, bf16[128,1024]{1,0:T(8,128)(2,1)} %bitcast.9), custom_call_target="tpu_custom_call" | custom-call | tf_op jit(solution)/shard_map/act/pallas_call | solution.py:173
  69.2 11.7 %all_to_all.25 = f32[32,8,128]{2,1,0:T(8,128)S(1)} all-to-all(f32[32,8,128]{2,1,0:T(8,128)} %act.1), channel_id=1, replica_groups={{0,8,16,24,32,40,48,56,2,10,18,26,34,42,50,58,4,12,20,28,36,44,52,60,6,..., dimensions={0} | all-to-all | bytes 262144 | tf_op jit(solution)/shard_map/all_to_all | solution.py:212
  81.0 0.1 reshape.30
  81.1 0.1 copy.15
  81.2 0.1 all_to_all.18
  81.3 13.8 %all_to_all.26 = f32[16,1,48]{2,1,0:T(1,128)S(1)} all-to-all(f32[16,1,48]{2,1,0:T(1,128)S(1)} %bitcast.10), channel_id=1, replica_groups={{0,64,128,192,256,320,384,448,1,65,129,193,257,321,385,449},{8,72,136,2..., dimensions={0} | all-to-all | bytes 6144 | tf_op jit(solution)/shard_map/all_to_all | solution.py:215
  95.2 0.6 reshape.31
  (7 shorter events, 0.1 us)
Async XLA Ops:
  0.0 0.7 copy-start.2
  0.0 0.8 copy-start.1
  29.9 23.4 %all-to-all-start.1 = ((bf16[32,96,128]{2,1,0:T(8,128)(2,1)}), bf16[32,96,128]{2,1,0:T(8,128)(2,1)S(1)}, u32[]{:S(2)}, u32[]{:S(2)}) async-start(bf16[32,96,128]{2,1,0:T(8,128)(2,1)} %swap.1), calls=%async_computation.1 | async-start | bytes 1572864 | tf_op jit(solution)/shard_map/all_to_all | solution.py:205
  53.2 0.9 copy-start

commit v2 on v1

v2 whole, which is shorter than its diff:
```python
import itertools

import jax
import jax.numpy as jnp
from jax import lax
from jax.experimental import pallas as pl
from jax.experimental.pallas import tpu as pltpu
from jax.sharding import PartitionSpec as P

AXES = ("pb", "wa")
NX, NY, NZ, NC = 4, 4, 16, 2
F32 = jnp.float32
BF16 = jnp.bfloat16
NT = (((1,), (1,)), ((), ()))


def place(x, y, z, c):
    return (((z % 8) * NX + x) * NC + c) * 8 + y * 2 + z // 8


def lines():
    spans = itertools.product(range(NX), range(NY), range(NC))
    return [[place(x, y, z, c) for z in range(NZ)] for x, y, c in spans]


def planes():
    spots = list(itertools.product(range(NY), range(NX), range(NC)))
    return [[place(x, y, z, c) for y, x, c in spots] for z in range(NZ)]


def sheets():
    spots = list(itertools.product(range(NY), range(NX)))
    spans = itertools.product(range(NZ), range(NC))
    return [[place(x, y, z, c) for y, x in spots] for z, c in spans]


def partners():
    return [(i, i ^ 8) for i in range(NX * NY * NZ * NC)]


def exchange(x, groups):
    return lax.all_to_all(x, AXES, 0, 0, tiled=True, axis_index_groups=groups)


def swap_kernel(in_ref, out_ref, wide):
    wide[...] = in_ref[...].astype(F32).reshape(128, 128)
    row = lax.broadcasted_iota(jnp.int32, (8, 128), 0)
    lane = lax.broadcasted_iota(jnp.int32, (8, 128), 1) // 16
    turn = lax.rem(row - lane + 8, 8)
    tiles = []
    for zh in range(2):
        for a in range(6):
            tile = wide[pl.ds(zh * 64 + a, 8, stride=8), :]
            done = jnp.where(turn == 0, tile, 0.0)
            for step in range(1, 8):
                moved = pltpu.roll(pltpu.roll(tile, step, 0), 128 - 16 * step, 1)
                done = jnp.where(turn == step, moved, done)
            tiles.append(done)
    block = jnp.concatenate(tiles, axis=0).astype(BF16)
    for dest in range(out_ref.shape[0]):
        out_ref[dest] = block


def swap(x):
    vmem = pl.BlockSpec(memory_space=pltpu.VMEM)
    return pl.pallas_call(
        swap_kernel,
        out_shape=jax.ShapeDtypeStruct((NX * NY, 96, 128), BF16),
        in_specs=[vmem],
        out_specs=vmem,
        scratch_shapes=[pltpu.VMEM((128, 128), F32)],
        compiler_params=pltpu.CompilerParams(vmem_limit_bytes=4 << 20),
        name="swap",
    )(x)


def main_kernel(
    kmap_ref, spot_ref, own_ref, other_ref, w_ref, o_ref,
    wt, psi, half, loc, t1, t2, mixed, wa, wb, acc, back,
):
    spot, core = spot_ref[0], spot_ref[1]
    lane16 = lax.broadcasted_iota(jnp.int32, (8, 128), 1) // 16
    own_row = lane16 == lax.broadcasted_iota(jnp.int32, (8, 128), 0)
    lane24 = lax.broadcasted_iota(jnp.int32, (24, 128), 1) // 16

    for z in range(8):
        turned = w_ref[:, z * 128 : (z + 1) * 128].astype(F32).T.astype(BF16)
        for xc in range(8):
            wt[xc * 128 + z * 16 : xc * 128 + (z + 1) * 16, :] = turned[
                xc * 16 : (xc + 1) * 16
            ]

    def spread_one(k, j):
        y, k4 = k // 4, lax.rem(k, 4)
        local = jnp.zeros((24, 128), F32)
        for x in range(4):
            for ref, c in ((own_ref, core), (other_ref, 1 - core)):
                xc = x * 2 + c
                tile16 = ref[y, x, k4]
                tile = tile16.astype(F32)
                lanes = pl.ds(pl.multiple_of(xc * 128, 128), 128)
                psi[k, :, lanes] = tile
                half[k, :, lanes] = tile16
                shift = lax.rem((xc - spot + 8) * 16, 128)
                local = jnp.where(lane24 == xc, pltpu.roll(tile, shift, 1), local)
        loc[k] = local
        rows, flat = [], []
        for u in range(8):
            for xh in range(2):
                xc = xh * 4 + u // 2
                at = psi[k, 12 + u % 2 : 13 + u % 2, xc * 128 : (xc + 1) * 128]
                rows.append(jnp.where(own_row, jnp.broadcast_to(at, (8, 128)), 0.0))
        left = jnp.concatenate(rows, axis=0).astype(BF16)
        right = jnp.concatenate([local[0:16].astype(BF16)] * 8, axis=0)
        first = jnp.dot(left, right, preferred_element_type=F32).astype(BF16)
        for u in range(8):
            t1[k, :, u * 128 : (u + 1) * 128] = first[u * 16 : (u + 1) * 16]
        flat = jnp.concatenate(
            [psi[k, 12:14, xc * 128 : (xc + 1) * 128] for xc in range(8)], axis=0
        )
        val = local[16:24].astype(BF16)
        none = jnp.zeros_like(val)
        right = jnp.concatenate(
            [
                jnp.concatenate([val, none], axis=1),
                jnp.concatenate([none, val], axis=1),
            ],
            axis=0,
        )
        second = jnp.dot(flat.T.astype(BF16), right, preferred_element_type=F32)
        for xh in range(2):
            mixed[j, xh] = second[:, xh * 128 : (xh + 1) * 128]
        for d in range(12):
            both = [mixed[j, xh, pl.ds(d, 8, stride=16), :] for xh in range(2)]
            t2[k, :, d * 128 : (d + 1) * 128] = jnp.concatenate(both, axis=0).astype(BF16)

    def spread(i, carry):
        for j in range(2):
            spread_one(i * 2 + j, j)
        return carry

    lax.fori_loop(0, 8, spread, 0)

    def grown(row):
        return jnp.broadcast_to(row, (16, row.shape[1])).astype(BF16)

    def pairs_of(k, j):
        p = kmap_ref[k]
        val_here = half[k, 16:24, :]
        val_here = jnp.concatenate([val_here, val_here], axis=0)
        cond_there = half[p, 0:16, :]
        parts = []
        for u in range(0, 8, 2):
            two = [
                jnp.broadcast_to(psi[p, 16 + u + i : 17 + u + i, :], (8, 1024))
                for i in range(2)
            ]
            parts.append(jnp.concatenate(two, axis=0).astype(BF16) * val_here)
        for d in range(12):
            parts.append(grown(psi[k, d : d + 1, :]) * cond_there)
        ww = jnp.dot(
            jnp.concatenate(parts, axis=0), wt[...], preferred_element_type=F32
        )
        wa[j] = ww[0:64]
        wb[j] = ww[64:256].astype(BF16)

    def close(k, j):
        p = kmap_ref[k]
        cond = loc[k, 0:16, :].astype(BF16)
        vals = [grown(loc[p, 16 + v : 17 + v, :]) for v in range(8)]
        lf = jnp.concatenate(
            [
                jnp.concatenate(
                    [grown(wa[j, u * 8 + v : u * 8 + v + 1, :]) * cond for v in range(8)],
                    axis=0,
                )
                for u in range(8)
            ],
            axis=1,
        )
        lb = jnp.concatenate(
            [
                jnp.concatenate(
                    [wb[j, d * 16 : (d + 1) * 16] * vals[v] for v in range(8)], axis=0
                )
                for d in range(12)
            ],
            axis=1,
        )
        acc[k] = lax.dot_general(t1[p], lf, NT, preferred_element_type=F32)
        back[p] = lax.dot_general(t2[k], lb, NT, preferred_element_type=F32)

    pairs_of(0, 0)

    def pair(i, carry):
        k = i * 2
        pairs_of(k + 1, 1)
        close(k, 0)
        pairs_of(lax.rem(k + 2, 16), 0)
        close(k + 1, 1)
        return carry

    lax.fori_loop(0, 8, pair, 0)

    lane32 = lax.broadcasted_iota(jnp.int32, (8, 128), 1) // 32
    for y in range(4):
        for xh in range(2):
            rows = slice(xh * 8, (xh + 1) * 8)
            held = [acc[y * 4 + i, rows] + back[y * 4 + i, rows] for i in range(4)]
            for vv in range(4):
                done = held[vv]
                for k4 in range(4):
                    if k4 != vv:
                        moved = pltpu.roll(held[k4], (k4 - vv) * 32 % 128, 1)
                        done = jnp.where(lane32 == k4, moved, done)
                o_ref[y * 8 + xh * 4 + vv] = done


def main(pairing, spot, own, other, weights):
    vmem = pl.BlockSpec(memory_space=pltpu.VMEM)
    smem = pl.BlockSpec(memory_space=pltpu.SMEM)
    return pl.pallas_call(
        main_kernel,
        out_shape=jax.ShapeDtypeStruct((32, 8, 128), F32),
        in_specs=[smem, smem, vmem, vmem, vmem],
        out_specs=vmem,
        scratch_shapes=[
            pltpu.VMEM((1024, 128), BF16),
            pltpu.VMEM((16, 24, 1024), F32),
            pltpu.VMEM((16, 24, 1024), BF16),
            pltpu.VMEM((16, 24, 128), F32),
            pltpu.VMEM((16, 16, 1024), BF16),
            pltpu.VMEM((16, 16, 1536), BF16),
            pltpu.VMEM((2, 2, 128, 128), F32),
            pltpu.VMEM((2, 64, 128), F32),
            pltpu.VMEM((2, 192, 128), BF16),
            pltpu.VMEM((16, 16, 128), F32),
            pltpu.VMEM((16, 16, 128), F32),
        ],
        compiler_params=pltpu.CompilerParams(vmem_limit_bytes=16 << 20),
        name="act",
    )(pairing, spot, own, other, weights)


def shards(psi_val, psi_cond, trials, screened, kmap):
    extra = jnp.pad(trials.reshape(2, 2, 12), ((0, 0), (0, 2), (0, 4)))
    line = jnp.concatenate([psi_cond, extra, psi_val], axis=1).reshape(6, 128)
    line = jnp.pad(line, ((0, 2), (0, 0)))
    along = exchange(jnp.broadcast_to(line, (16, 8, 128)), lines())
    own = exchange(swap(along), sheets())
    other = lax.ppermute(own, AXES, partners())
    spot = jnp.stack([lax.axis_index("wa"), lax.rem(lax.axis_index("pb"), 2)])
    shape = (4, 4, 4, 24, 128)
    sums = main(
        kmap.reshape(16), spot, own.reshape(shape), other.reshape(shape), screened[0]
    )
    sums = jnp.sum(exchange(sums, planes()), axis=0)
    sums = sums.reshape(8, 2, 64).transpose(1, 0, 2).reshape(16, 64)
    sums = jnp.sum(exchange(sums, lines()), axis=0)
    return sums.reshape(2, 2, 16)[:, :, :12].reshape(2, 24)


def solution(mesh):
    in_specs = (
        P("wa", None, "pb"),
        P("wa", None, "pb"),
        P("wa", "pb"),
        P("pb", "wa", None),
        P("pb", None),
    )
    return jax.shard_map(
        shards, mesh=mesh, in_specs=in_specs, out_specs=P("wa", "pb"), check_vma=False
    )
```

time: 96.3 us -> 86.9 us (0.902)
  blocking collectives: 52.7 us -> 66.7 us
  waiting for transfers between devices: 14.2 us -> 1.25 us
  Pallas kernels: 16.9 us -> 10 us
  starting transfers between devices: 9.13 us -> 5.34 us
    all_to_all x1 -> x0, waiting for transfers between devices: 14.2 us -> none  [shards(): lax.all_to_all(swap(along), AXES, 0, 0, tiled=True, axis_index_groups=pla...]
    all_to_all x3 -> x4, blocking collectives: 52.7 us -> 66.7 us  [exchange(): return lax.all_to_all(x, AXES, 0, 0, tiled=True, axis_index_groups=groups)]
    all_to_all x1 -> x0, starting transfers between devices: 9.13 us -> none  [shards(): lax.all_to_all(swap(along), AXES, 0, 0, tiled=True, axis_index_groups=pla...]
    ppermute x0 -> x1, starting transfers between devices: none -> 5.34 us  [shards(): other = lax.ppermute(own, AXES, partners())]
    pallas_call x1, Pallas kernels: 15.1 us -> 9.88 us  [main(): pl.pallas_call(main_kernel, out_shape=jax.ShapeDtypeStruct((32, 8, 128),...]
    pallas_call x1, Pallas kernels: 1.78 us -> 0.13 us  [swap(): pl.pallas_call(swap_kernel, out_shape=jax.ShapeDtypeStruct((NX * NY, 96,...]
    ppermute x0 -> x1, waiting for transfers between devices: none -> 1.25 us  [shards(): other = lax.ppermute(own, AXES, partners())]
where the time goes in v2:
time: 86.9 us; the launch traced here: 86.6 us
  blocking collectives  66.7 us (77%)
  Pallas kernels  10 us (12%)
  starting transfers between devices  5.34 us (6%)
  local copies, waits for them, and re-layouts  3.04 us (3%)
  waiting for transfers between devices  1.25 us (1%)
    all_to_all x4, blocking collectives, exchange(): return lax.all_to_all(x, AXES, 0, 0, tiled=True, axis_index_groups=groups)  66.7 us
    pallas_call x1, Pallas kernels, main(): pl.pallas_call(main_kernel, out_shape=jax.ShapeDtypeStruct((32, 8, 128),...  9.88 us
    ppermute x1, starting transfers between devices, shards(): other = lax.ppermute(own, AXES, partners())  5.34 us
  transfers between devices with their start and end apart: 1, of which 1 were waited for; matrix products, arithmetic and copies ran while one was open for 0% of the time, Pallas kernels for 0%

profile of v2, /device:TPU:1, one launch (start us, length us, event | category | flops | bytes accessed | tf_op | source)
XLA Modules:
  0.0 86.6 jit_solution(3064921472528286153)
XLA Ops:
  0.0 0.0 copy-start.2
  0.0 0.8 reshape.29
  0.8 0.7 copy.16
  1.5 0.0 copy-done.2
  1.5 0.1 reshape.30
  1.6 27.0 %all_to_all.24.in_ref = bf16[16,8,128]{2,1,0:T(8,128)(2,1)S(1)} all-to-all(bf16[16,8,128]{2,1,0:T(8,128)(2,1)S(1)} %broadcast_in_dim.3), channel_id=1, replica_groups={{0,64,128,192,256,320,384,448,1,65,129,193,257,321,385,449},{8,72,136,2..., dimensions={0} | all-to-all | bytes 65536 | tf_op jit(solution)/shard_map/all_to_all | solution.py:42
  28.6 0.1 swap.1
  28.7 0.0 copy-start
  28.8 15.0 %all_to_all.25 = bf16[16,96,128]{2,1,0:T(8,128)(2,1)S(1)} all-to-all(bf16[16,96,128]{2,1,0:T(8,128)(2,1)S(1)} %swap.1), channel_id=1, replica_groups={{0,16,32,48,2,18,34,50,4,20,36,52,6,22,38,54},{8,24,40,56,10,26,42,58,1..., dimensions={0} | all-to-all | bytes 786432 | tf_op jit(solution)/shard_map/all_to_all | solution.py:42
  43.7 5.3 %collective-permute-start = (bf16[16,96,128]{2,1,0:T(8,128)(2,1)S(1)}, bf16[16,96,128]{2,1,0:T(8,128)(2,1)S(1)}, u32[]{:S(2)}, u32[]{:S(2)}) collective-permute-start(bf16[16,96,128]{2,1,0:T(8,128)(2,1)S(1)} %all_to_all.25), channel_id=1, source_target_pairs={{0,8},{1,9},{2,10},{3,11},{4,12},{5,13},{6,14},{7,15},{8,0},{9,1},... | collective-permute-start | bytes 1179656 | tf_op jit(solution)/shard_map/ppermute | solution.py:251
  49.1 0.1 pad_add_fusion.spot_ref
  49.1 1.2 %collective-permute-done = bf16[16,96,128]{2,1,0:T(8,128)(2,1)S(1)} collective-permute-done((bf16[16,96,128]{2,1,0:T(8,128)(2,1)S(1)}, bf16[16,96,128]{2,1,0:T(8,128)(2,1)S(1)}, u32[]{:S(2)}, u32[]{:S(2)}) %collective-permute-start) | collective-permute-done | bytes 393248 | tf_op jit(solution)/shard_map/ppermute | solution.py:251
  50.4 0.0 copy-start.1
  50.4 0.0 copy-done
  50.4 0.7 copy-done.1
  51.1 9.9 %act.1 = f32[32,8,128]{2,1,0:T(8,128)S(1)} custom-call(s32[16]{0:T(128)S(1)} %bitcast.14, s32[2]{0:T(128)S(1)} %pad_add_fusion.spot_ref, bf16[4,4,4,24,128]{4,3,2,1,0:T(8,128)(2,1)S(1)} %bitcast.11, bf16[4,4,4,24,128]{4,3,2,1,0:T(8,128)(2,1)S(1)} %bitcast.12, bf16[128,1024]{1,0:T(8,128)(2,1)S(1)} %bitcast.13), custom_call_target="tpu_custom_call" | custom-call | tf_op jit(solution)/shard_map/act/pallas_call | solution.py:222
  60.9 10.9 %all_to_all.26 = f32[32,8,128]{2,1,0:T(8,128)S(1)} all-to-all(f32[32,8,128]{2,1,0:T(8,128)S(1)} %act.1), channel_id=1, replica_groups={{0,8,16,24,32,40,48,56,2,10,18,26,34,42,50,58,4,12,20,28,36,44,52,60,6,..., dimensions={0} | all-to-all | bytes 262144 | tf_op jit(solution)/shard_map/all_to_all | solution.py:42
  71.9 0.1 reshape.33
  72.0 13.8 %all_to_all.27 = f32[16,1,64]{2,1,0:T(1,128)S(1)} all-to-all(f32[16,1,64]{2,1,0:T(1,128)S(1)} %bitcast.16), channel_id=1, replica_groups={{0,64,128,192,256,320,384,448,1,65,129,193,257,321,385,449},{8,72,136,2..., dimensions={0} | all-to-all | bytes 8192 | tf_op jit(solution)/shard_map/all_to_all | solution.py:42
  85.9 0.1 reshape.34
  85.9 0.6 reshape.35
  (8 shorter events, 0.1 us)
Async XLA Ops:
  0.0 1.5 %copy-start.2 = (bf16[2,12,16]{2,0,1:T(2,128)(2,1)S(1)}, bf16[2,12,16]{2,0,1:T(2,128)(2,1)}, u32[]{:S(2)}) copy-start(bf16[2,12,16]{2,0,1:T(2,128)(2,1)} %param.6) | copy-start | bytes 2308
  28.7 21.7 %copy-start = (bf16[1,128,1024]{2,1,0:T(8,128)(2,1)S(1)}, bf16[1,128,1024]{2,1,0:T(8,128)(2,1)}, u32[]{:S(2)}) copy-start(bf16[1,128,1024]{2,1,0:T(8,128)(2,1)} %param.8) | copy-start | bytes 786436
  43.7 6.7 %collective-permute-start = (bf16[16,96,128]{2,1,0:T(8,128)(2,1)S(1)}, bf16[16,96,128]{2,1,0:T(8,128)(2,1)S(1)}, u32[]{:S(2)}, u32[]{:S(2)}) collective-permute-start(bf16[16,96,128]{2,1,0:T(8,128)(2,1)S(1)} %all_to_all.25), channel_id=1, source_target_pairs={{0,8},{1,9},{2,10},{3,11},{4,12},{5,13},{6,14},{7,15},{8,0},{9,1},... | collective-permute-start | bytes 1179656 | tf_op jit(solution)/shard_map/ppermute | solution.py:251
  50.4 0.7 copy-start.1

commit v3 on v2

--- a/solution.py
+++ b/solution.py
@@ -40,6 +40,54 @@
 
 def exchange(x, groups):
     return lax.all_to_all(x, AXES, 0, 0, tiled=True, axis_index_groups=groups)
+
+
+def line_kernel(val_in, cond_in, trial_in, out_ref, val_ref, cond_ref, trial_ref, wide, sems):
+    pairs = ((val_in, val_ref), (cond_in, cond_ref), (trial_in, trial_ref))
+    copies = [
+        pltpu.make_async_copy(there, here, sems.at[i])
+        for i, (there, here) in enumerate(pairs)
+    ]
+    for copy in copies:
+        copy.start()
+    wide[...] = jnp.zeros_like(wide)
+    for copy in copies:
+        copy.wait()
+    for k in range(2):
+        base = k * 24
+        for band in range(12):
+            wide[base + band : base + band + 1, 0:16] = cond_ref[
+                band, k : k + 1, :
+            ].astype(F32)
+        for half in range(2):
+            wide[base + 12 + half : base + 13 + half, 0:12] = trial_ref[
+                k : k + 1, half * 12 : half * 12 + 12
+            ].astype(F32)
+        wide[base + 16 : base + 24, 0:16] = val_ref[k].astype(F32)
+    line = wide[pl.ds(0, 6, stride=8), :]
+    for slot in range(1, 8):
+        line += pltpu.roll(wide[pl.ds(slot, 6, stride=8), :], slot * 16, 1)
+    block = jnp.concatenate([line, jnp.zeros((2, 128), F32)], axis=0).astype(BF16)
+    for dest in range(out_ref.shape[0]):
+        out_ref[dest] = block
+
+
+def lined(val, cond, trial):
+    there = pl.BlockSpec(memory_space=pltpu.HBM)
+    return pl.pallas_call(
+        line_kernel,
+        out_shape=jax.ShapeDtypeStruct((NZ, 8, 128), BF16),
+        in_specs=[there, there, there],
+        out_specs=pl.BlockSpec(memory_space=pltpu.VMEM),
+        scratch_shapes=[
+            pltpu.VMEM(val.shape, BF16),
+            pltpu.VMEM(cond.shape, BF16),
+            pltpu.VMEM(trial.shape, BF16),
+            pltpu.VMEM((48, 128), F32),
+            pltpu.SemaphoreType.DMA((3,)),
+        ],
+        name="line",
+    )(val, cond, trial)
 
 
 def swap_kernel(in_ref, out_ref, wide):
@@ -75,48 +123,58 @@
 
 
 def main_kernel(
-    kmap_ref, spot_ref, own_ref, other_ref, w_ref, o_ref,
-    wt, psi, half, loc, t1, t2, mixed, wa, wb, acc, back,
+    table_ref, own_ref, other_ref, w_ref, o_ref,
+    wt, psi, loc, t1, t2, mixed, wa, wb, acc, back,
 ):
-    spot, core = spot_ref[0], spot_ref[1]
+    spot, core = table_ref[16], table_ref[17]
     lane16 = lax.broadcasted_iota(jnp.int32, (8, 128), 1) // 16
     own_row = lane16 == lax.broadcasted_iota(jnp.int32, (8, 128), 0)
     lane24 = lax.broadcasted_iota(jnp.int32, (24, 128), 1) // 16
 
+    sides = (own_ref, other_ref)
+
+    def seat(xc):
+        return xc - xc % 2 + (core if xc % 2 == 0 else 1 - core)
+
     for z in range(8):
         turned = w_ref[:, z * 128 : (z + 1) * 128].astype(F32).T.astype(BF16)
         for xc in range(8):
-            wt[xc * 128 + z * 16 : xc * 128 + (z + 1) * 16, :] = turned[
-                xc * 16 : (xc + 1) * 16
-            ]
+            rows = pl.ds(pl.multiple_of(seat(xc) * 128 + z * 16, 16), 16)
+            wt[rows, :] = turned[xc * 16 : (xc + 1) * 16]
+
+    def bands(k, rows):
+        y, k4 = k // 4, lax.rem(k, 4)
+        return jnp.concatenate(
+            [sides[n % 2][y, n // 2, k4, rows, :] for n in range(8)], axis=1
+        )
 
     def spread_one(k, j):
         y, k4 = k // 4, lax.rem(k, 4)
         local = jnp.zeros((24, 128), F32)
         for x in range(4):
-            for ref, c in ((own_ref, core), (other_ref, 1 - core)):
-                xc = x * 2 + c
-                tile16 = ref[y, x, k4]
-                tile = tile16.astype(F32)
-                lanes = pl.ds(pl.multiple_of(xc * 128, 128), 128)
-                psi[k, :, lanes] = tile
-                half[k, :, lanes] = tile16
+            for near in range(2):
+                xc = x * 2 + (core if near == 0 else 1 - core)
+                tile = sides[near][y, x, k4].astype(F32)
+                psi[k, x * 2 + near] = tile
                 shift = lax.rem((xc - spot + 8) * 16, 128)
                 local = jnp.where(lane24 == xc, pltpu.roll(tile, shift, 1), local)
         loc[k] = local
-        rows, flat = [], []
+
+    def weigh_one(k, j):
+        local = loc[k]
+        rows = []
         for u in range(8):
             for xh in range(2):
                 xc = xh * 4 + u // 2
-                at = psi[k, 12 + u % 2 : 13 + u % 2, xc * 128 : (xc + 1) * 128]
-                rows.append(jnp.where(own_row, jnp.broadcast_to(at, (8, 128)), 0.0))
+                at = psi[k, seat(xc), pl.ds(12 + u % 2, 8, stride=0), :]
+                rows.append(jnp.where(own_row, at, 0.0))
         left = jnp.concatenate(rows, axis=0).astype(BF16)
         right = jnp.concatenate([local[0:16].astype(BF16)] * 8, axis=0)
         first = jnp.dot(left, right, preferred_element_type=F32).astype(BF16)
         for u in range(8):
             t1[k, :, u * 128 : (u + 1) * 128] = first[u * 16 : (u + 1) * 16]
         flat = jnp.concatenate(
-            [psi[k, 12:14, xc * 128 : (xc + 1) * 128] for xc in range(8)], axis=0
+            [psi[k, seat(xc), 12:14, :] for xc in range(8)], axis=0
         )
         val = local[16:24].astype(BF16)
         none = jnp.zeros_like(val)
@@ -135,43 +193,78 @@
             t2[k, :, d * 128 : (d + 1) * 128] = jnp.concatenate(both, axis=0).astype(BF16)
 
     def spread(i, carry):
-        for j in range(2):
-            spread_one(i * 2 + j, j)
+        for j in range(4):
+            spread_one(i * 4 + j, j)
         return carry
 
-    lax.fori_loop(0, 8, spread, 0)
-
-    def grown(row):
-        return jnp.broadcast_to(row, (16, row.shape[1])).astype(BF16)
+    lax.fori_loop(0, 4, spread, 0)
+
+    upper = lax.broadcasted_iota(jnp.int32, (8, 128), 0) >= 4
+
+    def same(at, row):
+        return at[pl.ds(row, 8, stride=0), :]
+
+    def grown(at, row):
+        one = same(at, row)
+        return jnp.concatenate([one, one], axis=0).astype(BF16)
 
     def pairs_of(k, j):
-        p = kmap_ref[k]
-        val_here = half[k, 16:24, :]
+        p = table_ref[k]
+        val_here = bands(k, slice(16, 24))
         val_here = jnp.concatenate([val_here, val_here], axis=0)
-        cond_there = half[p, 0:16, :]
-        parts = []
-        for u in range(0, 8, 2):
-            two = [
-                jnp.broadcast_to(psi[p, 16 + u + i : 17 + u + i, :], (8, 1024))
-                for i in range(2)
-            ]
-            parts.append(jnp.concatenate(two, axis=0).astype(BF16) * val_here)
-        for d in range(12):
-            parts.append(grown(psi[k, d : d + 1, :]) * cond_there)
+        low = bands(p, slice(0, 8))
+        low = jnp.concatenate([low, low], axis=0)
+        high = []
+        for n in range(8):
+            tile = psi[p, n, 8:16, :]
+            tile = jnp.where(upper, pltpu.roll(tile, 4, 0), tile)
+            high.append(jnp.concatenate([tile, tile], axis=0).astype(BF16))
+        high = jnp.concatenate(high, axis=1)
+
+        def twins(at, one, two):
+            return jnp.concatenate(
+                [
+                    jnp.concatenate(
+                        [same(psi.at[at, n], one), same(psi.at[at, n], two)], axis=0
+                    ).astype(BF16)
+                    for n in range(8)
+                ],
+                axis=1,
+            )
+
+        def fours(at, first):
+            wide = []
+            for n in range(8):
+                rows = [same(psi.at[at, n], first + i) for i in range(4)]
+                halves = [
+                    jnp.where(upper, rows[i + 1], rows[i]) for i in range(0, 4, 2)
+                ]
+                wide.append(jnp.concatenate(halves, axis=0).astype(BF16))
+            return jnp.concatenate(wide, axis=1)
+
+        parts = [twins(p, 16 + u, 17 + u) * val_here for u in range(0, 8, 2)]
+        parts += [twins(k, d, d + 1) * low for d in range(0, 12, 2)]
+        parts += [fours(k, d) * high for d in range(0, 12, 4)]
         ww = jnp.dot(
             jnp.concatenate(parts, axis=0), wt[...], preferred_element_type=F32
         )
         wa[j] = ww[0:64]
-        wb[j] = ww[64:256].astype(BF16)
+        for d in range(12):
+            tail = ww[160 + d // 2 * 8 : 168 + d // 2 * 8]
+            if d % 2:
+                tail = pltpu.roll(tail, 4, 0)
+            wb[j, d * 16 : (d + 1) * 16] = jnp.concatenate(
+                [ww[64 + d * 8 : 72 + d * 8], tail], axis=0
+            ).astype(BF16)
 
     def close(k, j):
-        p = kmap_ref[k]
+        p = table_ref[k]
         cond = loc[k, 0:16, :].astype(BF16)
-        vals = [grown(loc[p, 16 + v : 17 + v, :]) for v in range(8)]
+        vals = [grown(loc.at[p], 16 + v) for v in range(8)]
         lf = jnp.concatenate(
             [
                 jnp.concatenate(
-                    [grown(wa[j, u * 8 + v : u * 8 + v + 1, :]) * cond for v in range(8)],
+                    [grown(wa.at[j], u * 8 + v) * cond for v in range(8)],
                     axis=0,
                 )
                 for u in range(8)
@@ -190,17 +283,23 @@
         acc[k] = lax.dot_general(t1[p], lf, NT, preferred_element_type=F32)
         back[p] = lax.dot_general(t2[k], lb, NT, preferred_element_type=F32)
 
-    pairs_of(0, 0)
+    for k in range(16):
+        weigh_one(k, k % 8)
+        if k == 7:
+            pairs_of(0, 0)
 
     def pair(i, carry):
         k = i * 2
         pairs_of(k + 1, 1)
         close(k, 0)
-        pairs_of(lax.rem(k + 2, 16), 0)
+        pairs_of(k + 2, 0)
         close(k + 1, 1)
         return carry
 
-    lax.fori_loop(0, 8, pair, 0)
+    lax.fori_loop(0, 7, pair, 0)
+    pairs_of(15, 1)
+    close(14, 0)
+    close(15, 1)
 
     lane32 = lax.broadcasted_iota(jnp.int32, (8, 128), 1) // 32
     for y in range(4):
@@ -216,22 +315,21 @@
                 o_ref[y * 8 + xh * 4 + vv] = done
 
 
-def main(pairing, spot, own, other, weights):
+def main(table, own, other, weights):
     vmem = pl.BlockSpec(memory_space=pltpu.VMEM)
     smem = pl.BlockSpec(memory_space=pltpu.SMEM)
     return pl.pallas_call(
         main_kernel,
         out_shape=jax.ShapeDtypeStruct((32, 8, 128), F32),
-        in_specs=[smem, smem, vmem, vmem, vmem],
+        in_specs=[smem, vmem, vmem, vmem],
         out_specs=vmem,
         scratch_shapes=[
             pltpu.VMEM((1024, 128), BF16),
-            pltpu.VMEM((16, 24, 1024), F32),
-            pltpu.VMEM((16, 24, 1024), BF16),
+            pltpu.VMEM((16, 8, 24, 128), F32),
             pltpu.VMEM((16, 24, 128), F32),
             pltpu.VMEM((16, 16, 1024), BF16),
             pltpu.VMEM((16, 16, 1536), BF16),
-            pltpu.VMEM((2, 2, 128, 128), F32),
+            pltpu.VMEM((8, 2, 128, 128), F32),
             pltpu.VMEM((2, 64, 128), F32),
             pltpu.VMEM((2, 192, 128), BF16),
             pltpu.VMEM((16, 16, 128), F32),
@@ -239,20 +337,18 @@
         ],
         compiler_params=pltpu.CompilerParams(vmem_limit_bytes=16 << 20),
         name="act",
-    )(pairing, spot, own, other, weights)
+    )(table, own, other, weights)
 
 
 def shards(psi_val, psi_cond, trials, screened, kmap):
-    extra = jnp.pad(trials.reshape(2, 2, 12), ((0, 0), (0, 2), (0, 4)))
-    line = jnp.concatenate([psi_cond, extra, psi_val], axis=1).reshape(6, 128)
-    line = jnp.pad(line, ((0, 2), (0, 0)))
-    along = exchange(jnp.broadcast_to(line, (16, 8, 128)), lines())
+    along = exchange(lined(psi_val, psi_cond.transpose(1, 0, 2), trials), lines())
     own = exchange(swap(along), sheets())
     other = lax.ppermute(own, AXES, partners())
-    spot = jnp.stack([lax.axis_index("wa"), lax.rem(lax.axis_index("pb"), 2)])
+    spot = jnp.stack([lax.axis_index("wa"), lax.axis_index("pb") & 1])
+    table = jnp.concatenate([kmap.reshape(16), spot])
     shape = (4, 4, 4, 24, 128)
     sums = main(
-        kmap.reshape(16), spot, own.reshape(shape), other.reshape(shape), screened[0]
+        table, own.reshape(shape), other.reshape(shape), screened[0]
     )
     sums = jnp.sum(exchange(sums, planes()), axis=0)
     sums = sums.reshape(8, 2, 64).transpose(1, 0, 2).reshape(16, 64)

time: 86.9 us -> 84.3 us (0.970)
  local copies, waits for them, and re-layouts: 3.04 us -> 1.47 us
    pallas_call x1, Pallas kernels: 9.88 us -> 7.83 us  [main(): pl.pallas_call(main_kernel, out_shape=jax.ShapeDtypeStruct((32, 8, 128),...]
    pallas_call x0 -> x1, Pallas kernels: none -> 1.49 us  [lined(): pl.pallas_call(line_kernel, out_shape=jax.ShapeDtypeStruct((NZ, 8, 128),...]
where the time goes in v3:
time: 84.3 us; the launch traced here: 84 us
  blocking collectives  66.9 us (79%)
  Pallas kernels  9.45 us (11%)
  starting transfers between devices  5.34 us (6%)
  local copies, waits for them, and re-layouts  1.47 us (2%)
    all_to_all x4, blocking collectives, exchange(): return lax.all_to_all(x, AXES, 0, 0, tiled=True, axis_index_groups=groups)  66.9 us
    pallas_call x1, Pallas kernels, main(): pl.pallas_call(main_kernel, out_shape=jax.ShapeDtypeStruct((32, 8, 128),...  7.83 us
    ppermute x1, starting transfers between devices, shards(): other = lax.ppermute(own, AXES, partners())  5.34 us
  transfers between devices with their start and end apart: 1, of which 1 were waited for; matrix products, arithmetic and copies ran while one was open for 0% of the time, Pallas kernels for 0%

profile of v3, /device:TPU:1, one launch (start us, length us, event | category | flops | bytes accessed | tf_op | source)
XLA Modules:
  0.0 84.0 jit_solution(281153726025244612)
XLA Ops:
  0.0 1.5 %line.1 = bf16[16,8,128]{2,1,0:T(8,128)(2,1)} custom-call(bf16[2,8,16]{2,1,0:T(8,128)(2,1)} %val_in.1, bf16[12,2,16]{2,1,0:T(2,128)(2,1)} %bitcast.18, bf16[2,24]{1,0:T(2,128)(2,1)} %trial_in.1), custom_call_target="tpu_custom_call" | custom-call | tf_op jit(solution)/shard_map/line/pallas_call | solution.py:77
  1.5 27.2 %all_to_all.24.in_ref = bf16[16,8,128]{2,1,0:T(8,128)(2,1)S(1)} all-to-all(bf16[16,8,128]{2,1,0:T(8,128)(2,1)} %line.1), channel_id=1, replica_groups={{0,64,128,192,256,320,384,448,1,65,129,193,257,321,385,449},{8,72,136,2..., dimensions={0} | all-to-all | bytes 65536 | tf_op jit(solution)/shard_map/all_to_all | solution.py:42
  28.7 0.1 swap.1
  28.9 0.0 copy-start
  28.9 15.0 %all_to_all.25 = bf16[16,96,128]{2,1,0:T(8,128)(2,1)S(1)} all-to-all(bf16[16,96,128]{2,1,0:T(8,128)(2,1)S(1)} %swap.1), channel_id=1, replica_groups={{0,16,32,48,2,18,34,50,4,20,36,52,6,22,38,54},{8,24,40,56,10,26,42,58,1..., dimensions={0} | all-to-all | bytes 786432 | tf_op jit(solution)/shard_map/all_to_all | solution.py:42
  43.8 5.3 %collective-permute-start = (bf16[16,96,128]{2,1,0:T(8,128)(2,1)S(1)}, bf16[16,96,128]{2,1,0:T(8,128)(2,1)S(1)}, u32[]{:S(2)}, u32[]{:S(2)}) collective-permute-start(bf16[16,96,128]{2,1,0:T(8,128)(2,1)S(1)} %all_to_all.25), channel_id=1, source_target_pairs={{0,8},{1,9},{2,10},{3,11},{4,12},{5,13},{6,14},{7,15},{8,0},{9,1},... | collective-permute-start | bytes 1179656 | tf_op jit(solution)/shard_map/ppermute | solution.py:346
  49.2 0.0 copy-start.1
  49.2 0.6 copy-done.1
  49.8 0.1 pad_add_fusion.table_ref
  49.9 0.6 collective-permute-done
  50.5 0.0 copy-done
  50.5 7.8 %act.1 = f32[32,8,128]{2,1,0:T(8,128)S(1)} custom-call(s32[18]{0:T(128)S(1)} %pad_add_fusion.table_ref, bf16[4,4,4,24,128]{4,3,2,1,0:T(8,128)(2,1)S(1)} %bitcast.12, bf16[4,4,4,24,128]{4,3,2,1,0:T(8,128)(2,1)S(1)} %bitcast.13, bf16[128,1024]{1,0:T(8,128)(2,1)S(1)} %bitcast.14), custom_call_target="tpu_custom_call" | custom-call | tf_op jit(solution)/shard_map/act/pallas_call | solution.py:321
  58.3 10.9 %all_to_all.26 = f32[32,8,128]{2,1,0:T(8,128)S(1)} all-to-all(f32[32,8,128]{2,1,0:T(8,128)S(1)} %act.1), channel_id=1, replica_groups={{0,8,16,24,32,40,48,56,2,10,18,26,34,42,50,58,4,12,20,28,36,44,52,60,6,..., dimensions={0} | all-to-all | bytes 262144 | tf_op jit(solution)/shard_map/all_to_all | solution.py:42
  69.3 0.1 reshape.25
  69.4 13.8 %all_to_all.27 = f32[16,1,64]{2,1,0:T(1,128)S(1)} all-to-all(f32[16,1,64]{2,1,0:T(1,128)S(1)} %bitcast.16), channel_id=1, replica_groups={{0,64,128,192,256,320,384,448,1,65,129,193,257,321,385,449},{8,72,136,2..., dimensions={0} | all-to-all | bytes 8192 | tf_op jit(solution)/shard_map/all_to_all | solution.py:42
  83.3 0.1 reshape.26
  83.3 0.6 reshape.27
  (3 shorter events, 0.1 us)
Async XLA Ops:
  28.9 21.7 %copy-start = (bf16[1,128,1024]{2,1,0:T(8,128)(2,1)S(1)}, bf16[1,128,1024]{2,1,0:T(8,128)(2,1)}, u32[]{:S(2)}) copy-start(bf16[1,128,1024]{2,1,0:T(8,128)(2,1)} %param.8) | copy-start | bytes 786436
  43.8 6.7 %collective-permute-start = (bf16[16,96,128]{2,1,0:T(8,128)(2,1)S(1)}, bf16[16,96,128]{2,1,0:T(8,128)(2,1)S(1)}, u32[]{:S(2)}, u32[]{:S(2)}) collective-permute-start(bf16[16,96,128]{2,1,0:T(8,128)(2,1)S(1)} %all_to_all.25), channel_id=1, source_target_pairs={{0,8},{1,9},{2,10},{3,11},{4,12},{5,13},{6,14},{7,15},{8,0},{9,1},... | collective-permute-start | bytes 1179656 | tf_op jit(solution)/shard_map/ppermute | solution.py:346
  49.2 0.7 copy-start.1

commit v4 on v3

--- a/solution.py
+++ b/solution.py
@@ -143,13 +143,13 @@
             wt[rows, :] = turned[xc * 16 : (xc + 1) * 16]
 
     def bands(k, rows):
-        y, k4 = k // 4, lax.rem(k, 4)
+        y, k4 = divmod(k, 4) if isinstance(k, int) else (k // 4, lax.rem(k, 4))
         return jnp.concatenate(
             [sides[n % 2][y, n // 2, k4, rows, :] for n in range(8)], axis=1
         )
 
     def spread_one(k, j):
-        y, k4 = k // 4, lax.rem(k, 4)
+        y, k4 = divmod(k, 4) if isinstance(k, int) else (k // 4, lax.rem(k, 4))
         local = jnp.zeros((24, 128), F32)
         for x in range(4):
             for near in range(2):
@@ -163,16 +163,16 @@
     def weigh_one(k, j):
         local = loc[k]
         rows = []
-        for u in range(8):
-            for xh in range(2):
+        for xh in range(2):
+            for u in range(8):
                 xc = xh * 4 + u // 2
                 at = psi[k, seat(xc), pl.ds(12 + u % 2, 8, stride=0), :]
                 rows.append(jnp.where(own_row, at, 0.0))
         left = jnp.concatenate(rows, axis=0).astype(BF16)
         right = jnp.concatenate([local[0:16].astype(BF16)] * 8, axis=0)
-        first = jnp.dot(left, right, preferred_element_type=F32).astype(BF16)
-        for u in range(8):
-            t1[k, :, u * 128 : (u + 1) * 128] = first[u * 16 : (u + 1) * 16]
+        first = jnp.dot(left, right, preferred_element_type=F32)
+        for xh in range(2):
+            t1[k, xh] = first[xh * 64 : (xh + 1) * 64]
         flat = jnp.concatenate(
             [psi[k, seat(xc), 12:14, :] for xc in range(8)], axis=0
         )
@@ -197,7 +197,8 @@
             spread_one(i * 4 + j, j)
         return carry
 
-    lax.fori_loop(0, 4, spread, 0)
+    for i in range(4):
+        spread(i, 0)
 
     upper = lax.broadcasted_iota(jnp.int32, (8, 128), 0) >= 4
 
@@ -242,35 +243,54 @@
                 wide.append(jnp.concatenate(halves, axis=0).astype(BF16))
             return jnp.concatenate(wide, axis=1)
 
-        parts = [twins(p, 16 + u, 17 + u) * val_here for u in range(0, 8, 2)]
-        parts += [twins(k, d, d + 1) * low for d in range(0, 12, 2)]
-        parts += [fours(k, d) * high for d in range(0, 12, 4)]
-        ww = jnp.dot(
-            jnp.concatenate(parts, axis=0), wt[...], preferred_element_type=F32
-        )
-        wa[j] = ww[0:64]
-        for d in range(12):
-            tail = ww[160 + d // 2 * 8 : 168 + d // 2 * 8]
-            if d % 2:
-                tail = pltpu.roll(tail, 4, 0)
-            wb[j, d * 16 : (d + 1) * 16] = jnp.concatenate(
-                [ww[64 + d * 8 : 72 + d * 8], tail], axis=0
-            ).astype(BF16)
+        def some(i):
+            if i == 0:
+                return [twins(p, 16 + u, 17 + u) * val_here for u in range(0, 8, 2)]
+            if i == 1:
+                return [twins(k, d, d + 1) * low for d in range(0, 6, 2)] + [
+                    fours(k, 0) * high
+                ]
+            return [twins(k, d, d + 1) * low for d in range(6, 12, 2)] + [
+                fours(k, d) * high for d in (4, 8)
+            ]
+
+        def dot(i):
+            return jnp.dot(
+                jnp.concatenate(some(i), axis=0), wt[...], preferred_element_type=F32
+            )
+
+        def finish(got):
+            wa[j] = got[0]
+            for d in range(12):
+                piece = got[1] if d < 6 else got[2]
+                first = piece[d % 6 * 8 : d % 6 * 8 + 8]
+                if d < 4:
+                    tail = got[1][48 + d // 2 * 8 : 56 + d // 2 * 8]
+                else:
+                    tail = got[2][48 + (d - 4) // 2 * 8 : 56 + (d - 4) // 2 * 8]
+                if d % 2:
+                    tail = pltpu.roll(tail, 4, 0)
+                wb[j, d * 16 : (d + 1) * 16] = jnp.concatenate(
+                    [first, tail], axis=0
+                ).astype(BF16)
+
+        return some, finish
+
+    def pairs_two(k0, j0, k1, j1):
+        some0, finish0 = pairs_of(k0, j0)
+        some1, finish1 = pairs_of(k1, j1)
+        for some, finish in ((some0, finish0), (some1, finish1)):
+            got = jnp.dot(
+                jnp.concatenate(some(0) + some(1) + some(2), axis=0),
+                wt[...],
+                preferred_element_type=F32,
+            )
+            finish([got[0:64], got[64:128], got[128:208]])
 
     def close(k, j):
         p = table_ref[k]
         cond = loc[k, 0:16, :].astype(BF16)
         vals = [grown(loc.at[p], 16 + v) for v in range(8)]
-        lf = jnp.concatenate(
-            [
-                jnp.concatenate(
-                    [grown(wa.at[j], u * 8 + v) * cond for v in range(8)],
-                    axis=0,
-                )
-                for u in range(8)
-            ],
-            axis=1,
-        )
         lb = jnp.concatenate(
             [
                 jnp.concatenate(
@@ -280,26 +300,50 @@
             ],
             axis=1,
         )
-        acc[k] = lax.dot_general(t1[p], lf, NT, preferred_element_type=F32)
+        tiles = []
+        for xh in range(2):
+            for v in range(8):
+                total = same(wa.at[j], v) * t1[p, xh, 0:8, :]
+                for u in range(1, 8):
+                    total += same(wa.at[j], u * 8 + v) * t1[p, xh, u * 8 : u * 8 + 8, :]
+                tiles.append(total)
+        left = jnp.concatenate(tiles, axis=0).astype(BF16)
+        right = jnp.concatenate([cond, jnp.zeros((112, 128), BF16)], axis=0)
+        out = lax.dot_general(left, right, NT, preferred_element_type=F32)
+        for xh in range(2):
+            total = out[xh * 64 : xh * 64 + 8]
+            for v in range(1, 8):
+                at = xh * 64 + v * 8
+                total += pltpu.roll(out[at : at + 8], v * 16, 1)
+            acc[k, xh * 8 : (xh + 1) * 8, :] = total
         back[p] = lax.dot_general(t2[k], lb, NT, preferred_element_type=F32)
 
     for k in range(16):
         weigh_one(k, k % 8)
         if k == 7:
-            pairs_of(0, 0)
+            pairs_two(0, 0, 1, 1)
 
     def pair(i, carry):
-        k = i * 2
-        pairs_of(k + 1, 1)
-        close(k, 0)
-        pairs_of(k + 2, 0)
-        close(k + 1, 1)
+        k = i * 4
+        for n in range(4):
+            at, slot = k + 2 + n, (2 + n) % 4
+            some, finish = pairs_of(at, slot)
+            got = jnp.dot(
+                jnp.concatenate(some(0) + some(1) + some(2), axis=0),
+                wt[...],
+                preferred_element_type=F32,
+            )
+            finish([got[0:64], got[64:128], got[128:208]])
+            close(k + n, n)
         return carry
 
-    lax.fori_loop(0, 7, pair, 0)
-    pairs_of(15, 1)
-    close(14, 0)
-    close(15, 1)
+    for i in range(3):
+        pair(i, 0)
+    pairs_two(14, 2, 15, 3)
+    close(12, 0)
+    close(13, 1)
+    close(14, 2)
+    close(15, 3)
 
     lane32 = lax.broadcasted_iota(jnp.int32, (8, 128), 1) // 32
     for y in range(4):
@@ -327,11 +371,11 @@
             pltpu.VMEM((1024, 128), BF16),
             pltpu.VMEM((16, 8, 24, 128), F32),
             pltpu.VMEM((16, 24, 128), F32),
-            pltpu.VMEM((16, 16, 1024), BF16),
+            pltpu.VMEM((16, 2, 64, 128), F32),
             pltpu.VMEM((16, 16, 1536), BF16),
             pltpu.VMEM((8, 2, 128, 128), F32),
-            pltpu.VMEM((2, 64, 128), F32),
-            pltpu.VMEM((2, 192, 128), BF16),
+            pltpu.VMEM((4, 64, 128), F32),
+            pltpu.VMEM((4, 192, 128), BF16),
             pltpu.VMEM((16, 16, 128), F32),
             pltpu.VMEM((16, 16, 128), F32),
         ],

time: 84.3 us -> 82.1 us (0.974)
  Pallas kernels: 9.45 us -> 7.18 us
    pallas_call x1, Pallas kernels: 7.83 us -> 5.56 us  [main(): pl.pallas_call(main_kernel, out_shape=jax.ShapeDtypeStruct((32, 8, 128),...]
where the time goes in v4:
time: 82.1 us; the launch traced here: 81.7 us
  blocking collectives  67 us (82%)
  Pallas kernels  7.18 us (9%)
  starting transfers between devices  5.34 us (7%)
  local copies, waits for them, and re-layouts  1.47 us (2%)
    all_to_all x4, blocking collectives, exchange(): return lax.all_to_all(x, AXES, 0, 0, tiled=True, axis_index_groups=groups)  67 us
    pallas_call x1, Pallas kernels, main(): pl.pallas_call(main_kernel, out_shape=jax.ShapeDtypeStruct((32, 8, 128),...  5.56 us
    ppermute x1, starting transfers between devices, shards(): other = lax.ppermute(own, AXES, partners())  5.34 us
  transfers between devices with their start and end apart: 1, of which 1 were waited for; matrix products, arithmetic and copies ran while one was open for 0% of the time, Pallas kernels for 0%

profile of v4, /device:TPU:1, one launch (start us, length us, event | category | flops | bytes accessed | tf_op | source)
XLA Modules:
  0.0 81.7 jit_solution(16040790069245090480)
XLA Ops:
  0.0 1.5 %line.1 = bf16[16,8,128]{2,1,0:T(8,128)(2,1)} custom-call(bf16[2,8,16]{2,1,0:T(8,128)(2,1)} %val_in.1, bf16[12,2,16]{2,1,0:T(2,128)(2,1)} %bitcast.18, bf16[2,24]{1,0:T(2,128)(2,1)} %trial_in.1), custom_call_target="tpu_custom_call" | custom-call | tf_op jit(solution)/shard_map/line/pallas_call | solution.py:77
  1.5 27.2 %all_to_all.24.in_ref = bf16[16,8,128]{2,1,0:T(8,128)(2,1)S(1)} all-to-all(bf16[16,8,128]{2,1,0:T(8,128)(2,1)} %line.1), channel_id=1, replica_groups={{0,64,128,192,256,320,384,448,1,65,129,193,257,321,385,449},{8,72,136,2..., dimensions={0} | all-to-all | bytes 65536 | tf_op jit(solution)/shard_map/all_to_all | solution.py:42
  28.7 0.1 swap.1
  28.9 0.0 copy-start
  28.9 15.0 %all_to_all.25 = bf16[16,96,128]{2,1,0:T(8,128)(2,1)S(1)} all-to-all(bf16[16,96,128]{2,1,0:T(8,128)(2,1)S(1)} %swap.1), channel_id=1, replica_groups={{0,16,32,48,2,18,34,50,4,20,36,52,6,22,38,54},{8,24,40,56,10,26,42,58,1..., dimensions={0} | all-to-all | bytes 786432 | tf_op jit(solution)/shard_map/all_to_all | solution.py:42
  43.8 5.3 %collective-permute-start = (bf16[16,96,128]{2,1,0:T(8,128)(2,1)S(1)}, bf16[16,96,128]{2,1,0:T(8,128)(2,1)S(1)}, u32[]{:S(2)}, u32[]{:S(2)}) collective-permute-start(bf16[16,96,128]{2,1,0:T(8,128)(2,1)S(1)} %all_to_all.25), channel_id=1, source_target_pairs={{0,8},{1,9},{2,10},{3,11},{4,12},{5,13},{6,14},{7,15},{8,0},{9,1},... | collective-permute-start | bytes 1179656 | tf_op jit(solution)/shard_map/ppermute | solution.py:390
  49.2 0.0 copy-start.1
  49.2 0.6 copy-done.1
  49.8 0.1 pad_add_fusion.table_ref
  49.9 0.6 collective-permute-done
  50.5 0.0 copy-done
  50.5 5.6 %act.1 = f32[32,8,128]{2,1,0:T(8,128)S(1)} custom-call(s32[18]{0:T(128)S(1)} %pad_add_fusion.table_ref, bf16[4,4,4,24,128]{4,3,2,1,0:T(8,128)(2,1)S(1)} %bitcast.12, bf16[4,4,4,24,128]{4,3,2,1,0:T(8,128)(2,1)S(1)} %bitcast.13, bf16[128,1024]{1,0:T(8,128)(2,1)S(1)} %bitcast.14), custom_call_target="tpu_custom_call" | custom-call | tf_op jit(solution)/shard_map/act/pallas_call | solution.py:365
  56.1 10.9 %all_to_all.26 = f32[32,8,128]{2,1,0:T(8,128)S(1)} all-to-all(f32[32,8,128]{2,1,0:T(8,128)S(1)} %act.1), channel_id=1, replica_groups={{0,8,16,24,32,40,48,56,2,10,18,26,34,42,50,58,4,12,20,28,36,44,52,60,6,..., dimensions={0} | all-to-all | bytes 262144 | tf_op jit(solution)/shard_map/all_to_all | solution.py:42
  67.1 0.1 reshape.25
  67.1 13.8 %all_to_all.27 = f32[16,1,64]{2,1,0:T(1,128)S(1)} all-to-all(f32[16,1,64]{2,1,0:T(1,128)S(1)} %bitcast.16), channel_id=1, replica_groups={{0,64,128,192,256,320,384,448,1,65,129,193,257,321,385,449},{8,72,136,2..., dimensions={0} | all-to-all | bytes 8192 | tf_op jit(solution)/shard_map/all_to_all | solution.py:42
  81.0 0.1 reshape.26
  81.1 0.6 reshape.27
  (3 shorter events, 0.1 us)
Async XLA Ops:
  28.9 21.7 %copy-start = (bf16[1,128,1024]{2,1,0:T(8,128)(2,1)S(1)}, bf16[1,128,1024]{2,1,0:T(8,128)(2,1)}, u32[]{:S(2)}) copy-start(bf16[1,128,1024]{2,1,0:T(8,128)(2,1)} %param.8) | copy-start | bytes 786436
  43.8 6.7 %collective-permute-start = (bf16[16,96,128]{2,1,0:T(8,128)(2,1)S(1)}, bf16[16,96,128]{2,1,0:T(8,128)(2,1)S(1)}, u32[]{:S(2)}, u32[]{:S(2)}) collective-permute-start(bf16[16,96,128]{2,1,0:T(8,128)(2,1)S(1)} %all_to_all.25), channel_id=1, source_target_pairs={{0,8},{1,9},{2,10},{3,11},{4,12},{5,13},{6,14},{7,15},{8,0},{9,1},... | collective-permute-start | bytes 1179656 | tf_op jit(solution)/shard_map/ppermute | solution.py:390
  49.2 0.7 copy-start.1

commit v5 on v4

--- a/solution.py
+++ b/solution.py
@@ -86,8 +86,9 @@
             pltpu.VMEM((48, 128), F32),
             pltpu.SemaphoreType.DMA((3,)),
         ],
+        compiler_params=pltpu.CompilerParams(vmem_limit_bytes=4 << 20),
         name="line",
-    )(val, cond, trial)
+    )(*(pltpu.with_memory_space_constraint(a, pltpu.HBM) for a in (val, cond, trial)))
 
 
 def swap_kernel(in_ref, out_ref, wide):

time: 82.1 us -> 81.2 us (0.989)
  no operation moved by 1% of the time
where the time goes in v5:
time: 81.2 us; the launch traced here: 80.9 us
  blocking collectives  66.7 us (82%)
  Pallas kernels  6.59 us (8%)
  starting transfers between devices  5.34 us (7%)
  local copies, waits for them, and re-layouts  1.47 us (2%)
    all_to_all x4, blocking collectives, exchange(): return lax.all_to_all(x, AXES, 0, 0, tiled=True, axis_index_groups=groups)  66.7 us
    pallas_call x1, Pallas kernels, main(): pl.pallas_call(main_kernel, out_shape=jax.ShapeDtypeStruct((32, 8, 128),...  5.57 us
    ppermute x1, starting transfers between devices, shards(): other = lax.ppermute(own, AXES, partners())  5.34 us
  transfers between devices with their start and end apart: 1, of which 1 were waited for; matrix products, arithmetic and copies ran while one was open for 0% of the time, Pallas kernels for 0%

profile of v5, /device:TPU:1, one launch (start us, length us, event | category | flops | bytes accessed | tf_op | source)
XLA Modules:
  0.0 80.9 jit_solution(17853134358202904476)
XLA Ops:
  0.0 0.9 %line.1 = bf16[16,8,128]{2,1,0:T(8,128)(2,1)S(1)} custom-call(bf16[2,8,16]{2,1,0:T(8,128)(2,1)} %val_in.1, bf16[12,2,16]{2,1,0:T(2,128)(2,1)} %bitcast.18, bf16[2,24]{1,0:T(2,128)(2,1)} %trial_in.1), custom_call_target="tpu_custom_call" | custom-call | tf_op jit(solution)/shard_map/line/pallas_call | solution.py:77
  0.9 27.0 %all_to_all.24.in_ref = bf16[16,8,128]{2,1,0:T(8,128)(2,1)S(1)} all-to-all(bf16[16,8,128]{2,1,0:T(8,128)(2,1)S(1)} %line.1), channel_id=1, replica_groups={{0,64,128,192,256,320,384,448,1,65,129,193,257,321,385,449},{8,72,136,2..., dimensions={0} | all-to-all | bytes 65536 | tf_op jit(solution)/shard_map/all_to_all | solution.py:42
  27.9 0.1 swap.1
  28.0 0.0 copy-start
  28.1 15.0 %all_to_all.25 = bf16[16,96,128]{2,1,0:T(8,128)(2,1)S(1)} all-to-all(bf16[16,96,128]{2,1,0:T(8,128)(2,1)S(1)} %swap.1), channel_id=1, replica_groups={{0,16,32,48,2,18,34,50,4,20,36,52,6,22,38,54},{8,24,40,56,10,26,42,58,1..., dimensions={0} | all-to-all | bytes 786432 | tf_op jit(solution)/shard_map/all_to_all | solution.py:42
  43.0 5.3 %collective-permute-start = (bf16[16,96,128]{2,1,0:T(8,128)(2,1)S(1)}, bf16[16,96,128]{2,1,0:T(8,128)(2,1)S(1)}, u32[]{:S(2)}, u32[]{:S(2)}) collective-permute-start(bf16[16,96,128]{2,1,0:T(8,128)(2,1)S(1)} %all_to_all.25), channel_id=1, source_target_pairs={{0,8},{1,9},{2,10},{3,11},{4,12},{5,13},{6,14},{7,15},{8,0},{9,1},... | collective-permute-start | bytes 1179656 | tf_op jit(solution)/shard_map/ppermute | solution.py:391
  48.4 0.0 copy-start.1
  48.4 0.6 copy-done.1
  49.0 0.1 pad_add_fusion.table_ref
  49.1 0.6 collective-permute-done
  49.7 0.0 copy-done
  49.7 5.6 %act.1 = f32[32,8,128]{2,1,0:T(8,128)S(1)} custom-call(s32[18]{0:T(128)S(1)} %pad_add_fusion.table_ref, bf16[4,4,4,24,128]{4,3,2,1,0:T(8,128)(2,1)S(1)} %bitcast.12, bf16[4,4,4,24,128]{4,3,2,1,0:T(8,128)(2,1)S(1)} %bitcast.13, bf16[128,1024]{1,0:T(8,128)(2,1)S(1)} %bitcast.14), custom_call_target="tpu_custom_call" | custom-call | tf_op jit(solution)/shard_map/act/pallas_call | solution.py:366
  55.3 10.9 %all_to_all.26 = f32[32,8,128]{2,1,0:T(8,128)S(1)} all-to-all(f32[32,8,128]{2,1,0:T(8,128)S(1)} %act.1), channel_id=1, replica_groups={{0,8,16,24,32,40,48,56,2,10,18,26,34,42,50,58,4,12,20,28,36,44,52,60,6,..., dimensions={0} | all-to-all | bytes 262144 | tf_op jit(solution)/shard_map/all_to_all | solution.py:42
  66.2 0.1 reshape.25
  66.3 13.8 %all_to_all.27 = f32[16,1,64]{2,1,0:T(1,128)S(1)} all-to-all(f32[16,1,64]{2,1,0:T(1,128)S(1)} %bitcast.16), channel_id=1, replica_groups={{0,64,128,192,256,320,384,448,1,65,129,193,257,321,385,449},{8,72,136,2..., dimensions={0} | all-to-all | bytes 8192 | tf_op jit(solution)/shard_map/all_to_all | solution.py:42
  80.2 0.1 reshape.26
  80.3 0.6 reshape.27
  (3 shorter events, 0.1 us)
Async XLA Ops:
  28.0 21.7 %copy-start = (bf16[1,128,1024]{2,1,0:T(8,128)(2,1)S(1)}, bf16[1,128,1024]{2,1,0:T(8,128)(2,1)}, u32[]{:S(2)}) copy-start(bf16[1,128,1024]{2,1,0:T(8,128)(2,1)} %param.8) | copy-start | bytes 786436
  43.0 6.7 %collective-permute-start = (bf16[16,96,128]{2,1,0:T(8,128)(2,1)S(1)}, bf16[16,96,128]{2,1,0:T(8,128)(2,1)S(1)}, u32[]{:S(2)}, u32[]{:S(2)}) collective-permute-start(bf16[16,96,128]{2,1,0:T(8,128)(2,1)S(1)} %all_to_all.25), channel_id=1, source_target_pairs={{0,8},{1,9},{2,10},{3,11},{4,12},{5,13},{6,14},{7,15},{8,0},{9,1},... | collective-permute-start | bytes 1179656 | tf_op jit(solution)/shard_map/ppermute | solution.py:391
  48.4 0.7 copy-start.1

commit v6 on v5

--- a/solution.py
+++ b/solution.py
@@ -123,9 +123,34 @@
     )(x)
 
 
+def turn_kernel(table_ref, w_ref, out_ref):
+    core = table_ref[17]
+    for z in range(8):
+        turned = w_ref[:, z * 128 : (z + 1) * 128].astype(F32).T.astype(BF16)
+        for xc in range(8):
+            seat = xc - xc % 2 + (core if xc % 2 == 0 else 1 - core)
+            rows = pl.ds(pl.multiple_of(seat * 128 + z * 16, 16), 16)
+            out_ref[rows, :] = turned[xc * 16 : (xc + 1) * 16]
+
+
+def turn(table, weights):
+    vmem = pl.BlockSpec(memory_space=pltpu.VMEM)
+    return pl.pallas_call(
+        turn_kernel,
+        out_shape=jax.ShapeDtypeStruct((1024, 128), BF16),
+        in_specs=[pl.BlockSpec(memory_space=pltpu.SMEM), vmem],
+        out_specs=vmem,
+        compiler_params=pltpu.CompilerParams(vmem_limit_bytes=4 << 20),
+        cost_estimate=pl.CostEstimate(
+            flops=1 << 20, bytes_accessed=1 << 19, transcendentals=0
+        ),
+        name="turn",
+    )(table, weights)
+
+
 def main_kernel(
-    table_ref, own_ref, other_ref, w_ref, o_ref,
-    wt, psi, loc, t1, t2, mixed, wa, wb, acc, back,
+    table_ref, own_ref, other_ref, wt, o_ref,
+    psi, loc, t1, t2, mixed, wa, wb, acc, back,
 ):
     spot, core = table_ref[16], table_ref[17]
     lane16 = lax.broadcasted_iota(jnp.int32, (8, 128), 1) // 16
@@ -136,12 +161,6 @@
 
     def seat(xc):
         return xc - xc % 2 + (core if xc % 2 == 0 else 1 - core)
-
-    for z in range(8):
-        turned = w_ref[:, z * 128 : (z + 1) * 128].astype(F32).T.astype(BF16)
-        for xc in range(8):
-            rows = pl.ds(pl.multiple_of(seat(xc) * 128 + z * 16, 16), 16)
-            wt[rows, :] = turned[xc * 16 : (xc + 1) * 16]
 
     def bands(k, rows):
         y, k4 = divmod(k, 4) if isinstance(k, int) else (k // 4, lax.rem(k, 4))
@@ -188,9 +207,9 @@
         )
         second = jnp.dot(flat.T.astype(BF16), right, preferred_element_type=F32)
         for xh in range(2):
-            mixed[j, xh] = second[:, xh * 128 : (xh + 1) * 128]
-        for d in range(12):
-            both = [mixed[j, xh, pl.ds(d, 8, stride=16), :] for xh in range(2)]
+            mixed[k, xh] = second[:, xh * 128 : (xh + 1) * 128]
+        for d in range(6):
+            both = [mixed[k, xh, pl.ds(d, 8, stride=16), :] for xh in range(2)]
             t2[k, :, d * 128 : (d + 1) * 128] = jnp.concatenate(both, axis=0).astype(BF16)
 
     def spread(i, carry):
@@ -271,9 +290,7 @@
                     tail = got[2][48 + (d - 4) // 2 * 8 : 56 + (d - 4) // 2 * 8]
                 if d % 2:
                     tail = pltpu.roll(tail, 4, 0)
-                wb[j, d * 16 : (d + 1) * 16] = jnp.concatenate(
-                    [first, tail], axis=0
-                ).astype(BF16)
+                wb[j, d * 16 : (d + 1) * 16] = jnp.concatenate([first, tail], axis=0)
 
         return some, finish
 
@@ -292,15 +309,11 @@
         p = table_ref[k]
         cond = loc[k, 0:16, :].astype(BF16)
         vals = [grown(loc.at[p], 16 + v) for v in range(8)]
-        lb = jnp.concatenate(
-            [
-                jnp.concatenate(
-                    [wb[j, d * 16 : (d + 1) * 16] * vals[v] for v in range(8)], axis=0
-                )
-                for d in range(12)
-            ],
-            axis=1,
-        )
+        lb = []
+        for d in range(6):
+            row = wb[j, d * 16 : (d + 1) * 16].astype(BF16)
+            lb.append(jnp.concatenate([row * vals[v] for v in range(8)], axis=0))
+        lb = jnp.concatenate(lb, axis=1)
         tiles = []
         for xh in range(2):
             for v in range(8):
@@ -317,7 +330,31 @@
                 at = xh * 64 + v * 8
                 total += pltpu.roll(out[at : at + 8], v * 16, 1)
             acc[k, xh * 8 : (xh + 1) * 8, :] = total
-        back[p] = lax.dot_general(t2[k], lb, NT, preferred_element_type=F32)
+        part = lax.dot_general(t2[k], lb, NT, preferred_element_type=F32)
+        cols = [
+            [mixed[k, xh, pl.ds(d, 8, stride=16), :] for d in range(6, 12)]
+            for xh in range(2)
+        ]
+        tiles = []
+        for c in range(12):
+            rows = [same(wb.at[j], d * 16 + c) for d in range(6, 12)]
+            for xh in range(2):
+                total = rows[0] * cols[xh][0]
+                for one, two in zip(rows[1:], cols[xh][1:]):
+                    total += one * two
+                tiles.append(total)
+        left = jnp.concatenate(tiles, axis=0).astype(BF16)
+        val = loc[p, 16:24, :]
+        none = jnp.zeros((15, 128), F32)
+        right = [val[v : v + 1] if i == 0 else none for v in range(8) for i in range(2)]
+        right = jnp.concatenate(right, axis=0).astype(BF16)
+        out = lax.dot_general(left, right, NT, preferred_element_type=F32)
+        for xh in range(2):
+            total = part[xh * 8 : xh * 8 + 8] + out[xh * 8 : xh * 8 + 8]
+            for c in range(1, 12):
+                at = c * 16 + xh * 8
+                total += pltpu.roll(out[at : at + 8], c, 1)
+            back[p, xh * 8 : (xh + 1) * 8, :] = total
 
     for k in range(16):
         weigh_one(k, k % 8)
@@ -369,14 +406,13 @@
         in_specs=[smem, vmem, vmem, vmem],
         out_specs=vmem,
         scratch_shapes=[
-            pltpu.VMEM((1024, 128), BF16),
             pltpu.VMEM((16, 8, 24, 128), F32),
             pltpu.VMEM((16, 24, 128), F32),
             pltpu.VMEM((16, 2, 64, 128), F32),
-            pltpu.VMEM((16, 16, 1536), BF16),
-            pltpu.VMEM((8, 2, 128, 128), F32),
+            pltpu.VMEM((16, 16, 768), BF16),
+            pltpu.VMEM((16, 2, 128, 128), F32),
             pltpu.VMEM((4, 64, 128), F32),
-            pltpu.VMEM((4, 192, 128), BF16),
+            pltpu.VMEM((4, 192, 128), F32),
             pltpu.VMEM((16, 16, 128), F32),
             pltpu.VMEM((16, 16, 128), F32),
         ],
@@ -393,7 +429,7 @@
     table = jnp.concatenate([kmap.reshape(16), spot])
     shape = (4, 4, 4, 24, 128)
     sums = main(
-        table, own.reshape(shape), other.reshape(shape), screened[0]
+        table, own.reshape(shape), other.reshape(shape), turn(table, screened[0])
     )
     sums = jnp.sum(exchange(sums, planes()), axis=0)
     sums = sums.reshape(8, 2, 64).transpose(1, 0, 2).reshape(16, 64)

time: 81.2 us -> 80.9 us (level)
  transfers between devices with their start and end apart: 1 -> 1, of which waited for: 1 -> 0; matrix products, arithmetic and copies ran while one was open for 0% -> 0% of each run, Pallas kernels for 0% -> 1%
where the time goes in v6:
time: 80.9 us; the launch traced here: 80.6 us
  blocking collectives  66.6 us (82%)
  Pallas kernels  6.96 us (9%)
  starting transfers between devices  5.34 us (7%)
  local copies, waits for them, and re-layouts  1.47 us (2%)
    all_to_all x4, blocking collectives, exchange(): return lax.all_to_all(x, AXES, 0, 0, tiled=True, axis_index_groups=groups)  66.6 us
    ppermute x1, starting transfers between devices, shards(): other = lax.ppermute(own, AXES, partners())  5.34 us
    pallas_call x1, Pallas kernels, main(): pl.pallas_call(main_kernel, out_shape=jax.ShapeDtypeStruct((32, 8, 128),...  5.25 us
  transfers between devices with their start and end apart: 1, of which 0 were waited for; matrix products, arithmetic and copies ran while one was open for 0% of the time, Pallas kernels for 1%

profile of v6, /device:TPU:1, one launch (start us, length us, event | category | flops | bytes accessed | tf_op | source)
XLA Modules:
  0.0 80.6 jit_solution(15099109076921514500)
XLA Ops:
  0.0 0.9 %line.1 = bf16[16,8,128]{2,1,0:T(8,128)(2,1)S(1)} custom-call(bf16[2,8,16]{2,1,0:T(8,128)(2,1)} %val_in.1, bf16[12,2,16]{2,1,0:T(2,128)(2,1)} %bitcast.18, bf16[2,24]{1,0:T(2,128)(2,1)} %trial_in.1), custom_call_target="tpu_custom_call" | custom-call | tf_op jit(solution)/shard_map/line/pallas_call | solution.py:77
  0.9 27.0 %all_to_all.24.in_ref = bf16[16,8,128]{2,1,0:T(8,128)(2,1)S(1)} all-to-all(bf16[16,8,128]{2,1,0:T(8,128)(2,1)S(1)} %line.1), channel_id=1, replica_groups={{0,64,128,192,256,320,384,448,1,65,129,193,257,321,385,449},{8,72,136,2..., dimensions={0} | all-to-all | bytes 65536 | tf_op jit(solution)/shard_map/all_to_all | solution.py:42
  27.9 0.1 swap.1
  28.0 0.0 copy-start
  28.1 15.0 %all_to_all.25 = bf16[16,96,128]{2,1,0:T(8,128)(2,1)S(1)} all-to-all(bf16[16,96,128]{2,1,0:T(8,128)(2,1)S(1)} %swap.1), channel_id=1, replica_groups={{0,16,32,48,2,18,34,50,4,20,36,52,6,22,38,54},{8,24,40,56,10,26,42,58,1..., dimensions={0} | all-to-all | bytes 786432 | tf_op jit(solution)/shard_map/all_to_all | solution.py:42
  43.0 5.3 %collective-permute-start = (bf16[16,96,128]{2,1,0:T(8,128)(2,1)S(1)}, bf16[16,96,128]{2,1,0:T(8,128)(2,1)S(1)}, u32[]{:S(2)}, u32[]{:S(2)}) collective-permute-start(bf16[16,96,128]{2,1,0:T(8,128)(2,1)S(1)} %all_to_all.25), channel_id=1, source_target_pairs={{0,8},{1,9},{2,10},{3,11},{4,12},{5,13},{6,14},{7,15},{8,0},{9,1},... | collective-permute-start | bytes 1179656 | tf_op jit(solution)/shard_map/ppermute | solution.py:427
  48.4 0.0 copy-start.1
  48.4 0.6 copy-done.1
  49.0 0.1 pad_add_fusion.table_ref
  49.1 0.0 copy-done
  49.1 0.7 turn.1.wt
  49.8 0.0 collective-permute-done
  49.8 5.2 %act.1 = f32[32,8,128]{2,1,0:T(8,128)S(1)} custom-call(s32[18]{0:T(128)S(1)} %pad_add_fusion.table_ref, bf16[4,4,4,24,128]{4,3,2,1,0:T(8,128)(2,1)S(1)} %bitcast.12, bf16[4,4,4,24,128]{4,3,2,1,0:T(8,128)(2,1)S(1)} %bitcast.13, bf16[1024,128]{1,0:T(8,128)(2,1)S(1)} %turn.1.wt), custom_call_target="tpu_custom_call" | custom-call | tf_op jit(solution)/shard_map/act/pallas_call | solution.py:403
  55.1 10.8 %all_to_all.26 = f32[32,8,128]{2,1,0:T(8,128)S(1)} all-to-all(f32[32,8,128]{2,1,0:T(8,128)S(1)} %act.1), channel_id=1, replica_groups={{0,8,16,24,32,40,48,56,2,10,18,26,34,42,50,58,4,12,20,28,36,44,52,60,6,..., dimensions={0} | all-to-all | bytes 262144 | tf_op jit(solution)/shard_map/all_to_all | solution.py:42
  65.9 0.1 reshape.25
  66.0 13.8 %all_to_all.27 = f32[16,1,64]{2,1,0:T(1,128)S(1)} all-to-all(f32[16,1,64]{2,1,0:T(1,128)S(1)} %bitcast.16), channel_id=1, replica_groups={{0,64,128,192,256,320,384,448,1,65,129,193,257,321,385,449},{8,72,136,2..., dimensions={0} | all-to-all | bytes 8192 | tf_op jit(solution)/shard_map/all_to_all | solution.py:42
  79.9 0.1 reshape.26
  79.9 0.6 reshape.27
  (3 shorter events, 0.1 us)
Async XLA Ops:
  28.0 21.1 %copy-start = (bf16[1,128,1024]{2,1,0:T(8,128)(2,1)S(1)}, bf16[1,128,1024]{2,1,0:T(8,128)(2,1)}, u32[]{:S(2)}) copy-start(bf16[1,128,1024]{2,1,0:T(8,128)(2,1)} %param.8) | copy-start | bytes 786436
  43.0 6.8 %collective-permute-start = (bf16[16,96,128]{2,1,0:T(8,128)(2,1)S(1)}, bf16[16,96,128]{2,1,0:T(8,128)(2,1)S(1)}, u32[]{:S(2)}, u32[]{:S(2)}) collective-permute-start(bf16[16,96,128]{2,1,0:T(8,128)(2,1)S(1)} %all_to_all.25), channel_id=1, source_target_pairs={{0,8},{1,9},{2,10},{3,11},{4,12},{5,13},{6,14},{7,15},{8,0},{9,1},... | collective-permute-start | bytes 1179656 | tf_op jit(solution)/shard_map/ppermute | solution.py:427
  48.4 0.7 copy-start.1

commit v7 on v6

--- a/solution.py
+++ b/solution.py
@@ -24,8 +24,8 @@
 
 
 def planes():
-    spots = list(itertools.product(range(NY), range(NX), range(NC)))
-    return [[place(x, y, z, c) for y, x, c in spots] for z in range(NZ)]
+    spots = list(itertools.product(range(NX), range(NY), range(NC)))
+    return [[place(x, y, z, c) for x, y, c in spots] for z in range(NZ)]
 
 
 def sheets():
@@ -394,7 +394,7 @@
                     if k4 != vv:
                         moved = pltpu.roll(held[k4], (k4 - vv) * 32 % 128, 1)
                         done = jnp.where(lane32 == k4, moved, done)
-                o_ref[y * 8 + xh * 4 + vv] = done
+                o_ref[(xh * 2 + vv // 2) * 8 + y * 2 + vv % 2] = done
 
 
 def main(table, own, other, weights):

time: 80.9 us -> 81 us (level)
  no operation moved by 1% of the time
where the time goes in v7:
time: 81 us; the launch traced here: 80.7 us
  blocking collectives  66.7 us (82%)
  Pallas kernels  6.95 us (9%)
  starting transfers between devices  5.34 us (7%)
  local copies, waits for them, and re-layouts  1.47 us (2%)
    all_to_all x4, blocking collectives, exchange(): return lax.all_to_all(x, AXES, 0, 0, tiled=True, axis_index_groups=groups)  66.7 us
    ppermute x1, starting transfers between devices, shards(): other = lax.ppermute(own, AXES, partners())  5.34 us
    pallas_call x1, Pallas kernels, main(): pl.pallas_call(main_kernel, out_shape=jax.ShapeDtypeStruct((32, 8, 128),...  5.24 us
  transfers between devices with their start and end apart: 1, of which 0 were waited for; matrix products, arithmetic and copies ran while one was open for 0% of the time, Pallas kernels for 1%

profile of v7, /device:TPU:1, one launch (start us, length us, event | category | flops | bytes accessed | tf_op | source)
XLA Modules:
  0.0 80.7 jit_solution(6772733208241038850)
XLA Ops:
  0.0 0.9 %line.1 = bf16[16,8,128]{2,1,0:T(8,128)(2,1)S(1)} custom-call(bf16[2,8,16]{2,1,0:T(8,128)(2,1)} %val_in.1, bf16[12,2,16]{2,1,0:T(2,128)(2,1)} %bitcast.18, bf16[2,24]{1,0:T(2,128)(2,1)} %trial_in.1), custom_call_target="tpu_custom_call" | custom-call | tf_op jit(solution)/shard_map/line/pallas_call | solution.py:77
  0.9 27.0 %all_to_all.24.in_ref = bf16[16,8,128]{2,1,0:T(8,128)(2,1)S(1)} all-to-all(bf16[16,8,128]{2,1,0:T(8,128)(2,1)S(1)} %line.1), channel_id=1, replica_groups={{0,64,128,192,256,320,384,448,1,65,129,193,257,321,385,449},{8,72,136,2..., dimensions={0} | all-to-all | bytes 65536 | tf_op jit(solution)/shard_map/all_to_all | solution.py:42
  27.9 0.1 swap.1
  28.0 0.0 copy-start
  28.1 15.0 %all_to_all.25 = bf16[16,96,128]{2,1,0:T(8,128)(2,1)S(1)} all-to-all(bf16[16,96,128]{2,1,0:T(8,128)(2,1)S(1)} %swap.1), channel_id=1, replica_groups={{0,16,32,48,2,18,34,50,4,20,36,52,6,22,38,54},{8,24,40,56,10,26,42,58,1..., dimensions={0} | all-to-all | bytes 786432 | tf_op jit(solution)/shard_map/all_to_all | solution.py:42
  43.0 5.3 %collective-permute-start = (bf16[16,96,128]{2,1,0:T(8,128)(2,1)S(1)}, bf16[16,96,128]{2,1,0:T(8,128)(2,1)S(1)}, u32[]{:S(2)}, u32[]{:S(2)}) collective-permute-start(bf16[16,96,128]{2,1,0:T(8,128)(2,1)S(1)} %all_to_all.25), channel_id=1, source_target_pairs={{0,8},{1,9},{2,10},{3,11},{4,12},{5,13},{6,14},{7,15},{8,0},{9,1},... | collective-permute-start | bytes 1179656 | tf_op jit(solution)/shard_map/ppermute | solution.py:427
  48.4 0.0 copy-start.1
  48.4 0.6 copy-done.1
  49.0 0.1 pad_add_fusion.table_ref
  49.1 0.0 copy-done
  49.1 0.7 turn.1.wt
  49.8 0.0 collective-permute-done
  49.8 5.2 %act.1 = f32[32,8,128]{2,1,0:T(8,128)S(1)} custom-call(s32[18]{0:T(128)S(1)} %pad_add_fusion.table_ref, bf16[4,4,4,24,128]{4,3,2,1,0:T(8,128)(2,1)S(1)} %bitcast.12, bf16[4,4,4,24,128]{4,3,2,1,0:T(8,128)(2,1)S(1)} %bitcast.13, bf16[1024,128]{1,0:T(8,128)(2,1)S(1)} %turn.1.wt), custom_call_target="tpu_custom_call" | custom-call | tf_op jit(solution)/shard_map/act/pallas_call | solution.py:403
  55.1 10.9 %all_to_all.26 = f32[32,8,128]{2,1,0:T(8,128)S(1)} all-to-all(f32[32,8,128]{2,1,0:T(8,128)S(1)} %act.1), channel_id=1, replica_groups={{0,8,2,10,4,12,6,14,16,24,18,26,20,28,22,30,32,40,34,42,36,44,38,46,48,..., dimensions={0} | all-to-all | bytes 262144 | tf_op jit(solution)/shard_map/all_to_all | solution.py:42
  66.0 0.1 reshape.25
  66.1 13.8 %all_to_all.27 = f32[16,1,64]{2,1,0:T(1,128)S(1)} all-to-all(f32[16,1,64]{2,1,0:T(1,128)S(1)} %bitcast.16), channel_id=1, replica_groups={{0,64,128,192,256,320,384,448,1,65,129,193,257,321,385,449},{8,72,136,2..., dimensions={0} | all-to-all | bytes 8192 | tf_op jit(solution)/shard_map/all_to_all | solution.py:42
  79.9 0.1 reshape.26
  80.0 0.6 reshape.27
  (3 shorter events, 0.1 us)
Async XLA Ops:
  28.0 21.1 %copy-start = (bf16[1,128,1024]{2,1,0:T(8,128)(2,1)S(1)}, bf16[1,128,1024]{2,1,0:T(8,128)(2,1)}, u32[]{:S(2)}) copy-start(bf16[1,128,1024]{2,1,0:T(8,128)(2,1)} %param.8) | copy-start | bytes 786436
  43.0 6.8 %collective-permute-start = (bf16[16,96,128]{2,1,0:T(8,128)(2,1)S(1)}, bf16[16,96,128]{2,1,0:T(8,128)(2,1)S(1)}, u32[]{:S(2)}, u32[]{:S(2)}) collective-permute-start(bf16[16,96,128]{2,1,0:T(8,128)(2,1)S(1)} %all_to_all.25), channel_id=1, source_target_pairs={{0,8},{1,9},{2,10},{3,11},{4,12},{5,13},{6,14},{7,15},{8,0},{9,1},... | collective-permute-start | bytes 1179656 | tf_op jit(solution)/shard_map/ppermute | solution.py:427
  48.4 0.7 copy-start.1
